TPU v7x, 128 devices: a whole 4x4x4 slice. The times are simulated.
128 devices in a mesh: leaf: 64 (over z, y, x), front: 2 (over core).
Axes of the slice: x: 4, y: 4, z: 4, core: 2. Of those that a mesh axis runs over, the one named last changes fastest.
Arguments:
- fac_left: bfloat16 [64, 1536, 512], P('leaf', None, 'front'), may hold values from -6 to 6
- fac_right: bfloat16 [64, 256, 512], P('leaf', None, 'front'), may hold values from -0.21875 to 0.21875
- block_rank: int32 [64, 8], replicated, may hold values from 8 to 64
- col_map: int32 [64, 8], replicated, may hold values from 0 to 15, as said below
- child_lead: bfloat16 [64, 1536, 1536], P('leaf', 'front'), as said below
- orig_lead: bfloat16 [64, 768, 1536], P('leaf', 'front'), as said below
- orig_panel: bfloat16 [64, 1536, 2048], P('leaf', None, 'front'), may hold values from -4 to 4
- orig_next: bfloat16 [64, 512, 2048], P('leaf', None, 'front'), may hold values from -6 to 6
Outputs:
- factor_lead: float32 [64, 768, 1536], P('leaf', 'front')
- upper_panel: float32 [64, 1536, 2048], P('leaf', None, 'front')
- next_panel: float32 [64, 512, 2048], P('leaf', None, 'front')
Inputs may be any that keep to these rules, and one draw needn't show every extreme that they name: `col_map`: each child's 8 block columns name distinct parent block columns. `child_lead`: symmetric; with orig_lead it makes each parent's fully summed block positive definite. `orig_lead`: the two row halves of a parent form a symmetric matrix.
All inputs are finite; a program needn't handle non-finite values.
Results may differ from a plain program's by a relative error of at most 0.0049.
Values may be sent and summed in bfloat16 or wider, within the bound.
A program may use at most 192 MiB of HBM per device.

v0:
```python
import jax
import jax.numpy as jnp
from jax import lax
from jax.sharding import PartitionSpec as P

RMAX = 64
NEXTB = 2


def partner_2(value, axis, bit):
    mask = 2**bit
    pairs = [(source, source ^ mask) for source in range(lax.axis_size(axis))]
    return lax.ppermute(value, axis, pairs)


def spread_2(block, axis, source):
    block = jnp.where(lax.axis_index(axis) == source, block, jnp.zeros_like(block))
    return lax.psum(block, axis)


def shortened(value):

    def short(part):
        return part.astype(jnp.bfloat16) if part.dtype == jnp.float32 else part

    return jax.tree.map(short, value)


def expand_blocks(lefts, rights, ranks, rank_cap):
    count = ranks.shape[0]
    order = lefts.shape[0]
    width = rights.shape[0]
    mask = (jnp.arange(rank_cap)[None, :] < ranks[:, None]).astype(jnp.bfloat16)
    xs_part = lefts.reshape(order, count, rank_cap) * mask[None]
    ys_part = rights.reshape(width, count, rank_cap)
    dense = jnp.einsum("fnr,bnr->fnb", xs_part, ys_part, preferred_element_type=jnp.float32)
    return dense.astype(jnp.bfloat16).reshape(order, count * width)


def shards(fac_left, fac_right, block_rank, col_map, child_lead, orig_lead, orig_panel, orig_next):
    nfront = lax.axis_size("front")
    findex = lax.axis_index("front")
    lindex = lax.axis_index("leaf")
    order = fac_left.shape[1]
    width = fac_right.shape[1]
    rank_cap = RMAX
    next_cols = NEXTB * width
    half_next = next_cols // 2
    local_blocks = fac_left.shape[2] // rank_cap
    own_blocks = orig_panel.shape[2] // width
    parent_blocks = own_blocks * nfront * 2
    parity = lindex % 2
    is_even = parity == 0
    own_ranks = lax.dynamic_slice(block_rank, (lindex, findex * local_blocks), (1, local_blocks))[0]
    payload = expand_blocks(fac_left[0], fac_right[0], own_ranks, rank_cap)
    partner = lindex + 1 - 2 * parity
    near_pay, near_lead, near_orig = partner_2((payload, child_lead, orig_lead), "leaf", 0)
    panel_local = orig_panel[0]
    next_local = orig_next[0]
    top_orig = jnp.where(is_even, orig_lead, near_orig)
    low_orig = jnp.where(is_even, near_orig, orig_lead)
    gathered = (
        lax.all_gather(child_lead, "front", axis=1, tiled=True),
        lax.all_gather(near_lead, "front", axis=1, tiled=True),
        lax.all_gather(top_orig, "front", axis=1, tiled=True),
        lax.all_gather(low_orig, "front", axis=1, tiled=True),
    )
    lead = gathered[0][0].astype(jnp.float32) + gathered[1][0].astype(jnp.float32)
    lead = lead + jnp.concatenate([gathered[2][0], gathered[3][0]], axis=0).astype(jnp.float32)
    factor = jnp.linalg.cholesky(lead)
    owned = (
        parity * (parent_blocks // 2)
        + findex * own_blocks
        + jnp.arange(own_blocks, dtype=jnp.int32)
    )
    own_count = owned.shape[0]
    children = jnp.stack([lindex, partner])
    maps = col_map[children]
    stacked = jnp.stack([payload, near_pay])
    piece = lax.all_gather(stacked, "front", axis=2, tiled=True)
    count = piece.shape[2] // width
    blocks = piece.reshape(2, order, count, width)
    select = (maps[:, :, None] == owned[None, None, :]).astype(jnp.bfloat16)
    spread = jnp.einsum("cno,cfnb->fob", select, blocks, preferred_element_type=jnp.float32)
    assembled = panel_local.astype(jnp.float32) + spread.reshape(order, own_count * width)
    upper = jax.scipy.linalg.solve_triangular(factor, assembled, lower=True)
    own_leading = spread_2(upper[:, :half_next].astype(jnp.bfloat16), "front", 0).astype(
        jnp.float32
    )
    partner_rows = partner_2(shortened(own_leading), "leaf", 0).astype(own_leading.dtype)
    leading = jnp.concatenate(
        [
            jnp.where(is_even, own_leading, partner_rows),
            jnp.where(is_even, partner_rows, own_leading),
        ],
        axis=1,
    )
    updated = next_local.astype(jnp.float32) - jnp.dot(
        leading.T, upper, precision=lax.Precision.HIGHEST
    )
    row_count = order // 2 // nfront
    out_lead = lax.dynamic_slice_in_dim(
        factor, parity * (order // 2) + findex * row_count, row_count, 0
    )
    return (out_lead[None], upper[None], updated[None])


def solution(mesh):
    placed = (
        P("leaf", None, "front"),
        P("leaf", None, "front"),
        P(),
        P(),
        P("leaf", "front", None),
        P("leaf", "front", None),
        P("leaf", None, "front"),
        P("leaf", None, "front"),
    )
    return jax.shard_map(
        shards,
        mesh=mesh,
        in_specs=placed,
        out_specs=(P("leaf", "front", None), P("leaf", None, "front"), P("leaf", None, "front")),
        check_vma=False,
    )
```

profile of v0, /device:TPU:1, one launch (start us, length us, event | category | flops | bytes accessed | tf_op | source)
XLA Modules:
  0.0 858.9 jit_solution(9586873713373207598)
XLA Ops:
  11.2 25.3 %collective-permute-done.1 = bf16[1,384,1536]{1,2,0:T(8,128)(2,1)} collective-permute-done((bf16[1,384,1536]{1,2,0:T(8,128)(2,1)S(1)}, bf16[1,384,1536]{1,2,0:T(8,128)(2,1)}, u32[]{:S(2)}, u32[]{:S(2)}) %collective-permute-start.1) | collective-permute-done | bytes 1179680 | tf_op jit(solution)/shard_map/ppermute | solution.py:13
  44.6 49.9 %collective-permute-done = bf16[1,768,1536]{1,2,0:T(8,128)(2,1)S(1)} collective-permute-done((bf16[1,768,1536]{1,2,0:T(8,128)(2,1)}, bf16[1,768,1536]{1,2,0:T(8,128)(2,1)S(1)}, u32[]{:S(2)}, u32[]{:S(2)}) %collective-permute-start) | collective-permute-done | bytes 2359328 | tf_op jit(solution)/shard_map/ppermute | solution.py:13
  104.1 65.0 %collective-permute-done.2 = bf16[1536,1024]{0,1:T(8,128)(2,1)} collective-permute-done((bf16[1536,1024]{0,1:T(8,128)(2,1)S(1)}, bf16[1536,1024]{0,1:T(8,128)(2,1)}, u32[]{:S(2)}, u32[]{:S(2)}) %collective-permute-start.2) | collective-permute-done | bytes 3145760 | tf_op jit(solution)/shard_map/ppermute | solution.py:13
  169.1 5.2 pad_maximum_fusion
  174.5 10.5 %bitcast_add_fusion.1 = f32[1536,1536]{0,1:T(8,128)} fusion(bf16[1,1536,1536]{1,2,0:T(8,128)(2,1)} %all-gather.8.cloned.1.call-done, bf16[1,1536,1536]{1,2,0:T(8,128)(2,1)} %all-gather.6.cloned.1.call-done, bf16[768,1536]{0,1:T(8,128)(2,1)} %bitcast.197, bf16[768,1536]{0,1:T(8,128)(2,1)} %bitcast.196), kind=kLoop, calls=%fused_computation.5 | loop fusion | flops 18874368 | bytes 23592960 | tf_op jit(solution)/shard_map/add | solution.py:69
  184.9 10.7 %copy.26 = f32[1536,1536]{1,0:T(8,128)} copy(f32[1536,1536]{0,1:T(8,128)} %bitcast_add_fusion.1) | data formatting | bytes 18874368 | tf_op jit(solution)/shard_map/add | solution.py:69
  195.6 15.0 %fusion = f32[1536,1536]{1,0:T(8,128)} fusion(f32[1536,1536]{1,0:T(8,128)} %copy.26, f32[1536,1536]{0,1:T(8,128)} %bitcast_add_fusion.1), kind=kLoop, calls=%fused_computation.4 | loop fusion | flops 4718592 | bytes 28311552 | tf_op jit(solution)/shard_map/jit(cholesky)/div | solution.py:70
  211.5 11.7 %cholesky.341 = f32[128,128]{1,0:T(8,128)S(1)} custom-call(f32[128,128]{1,0:T(8,128)S(1)} %cholesky.892), custom_call_target="Cholesky" | custom-call | tf_op jit(solution)/shard_map/jit(cholesky)/cholesky | solution.py:70
  223.2 9.8 %custom-call.95 = f32[1,128,128]{1,2,0:T(8,128)S(1)} custom-call(f32[1,128,128]{2,1,0:T(8,128)S(1)} %get-tuple-element.127), custom_call_target="InvertDiagBlocksLowerTriangular" | custom-call | tf_op jit(solution)/shard_map/jit(cholesky)/cholesky | solution.py:70
  233.0 4.8 cholesky.371
  242.4 11.9 %cholesky.362 = f32[128,128]{1,0:T(8,128)S(1)} custom-call(f32[128,128]{1,0:T(8,128)S(1)} %cholesky.896), custom_call_target="Cholesky" | custom-call | tf_op jit(solution)/shard_map/jit(cholesky)/cholesky | solution.py:70
  255.0 9.8 %custom-call.96 = f32[1,128,128]{1,2,0:T(8,128)S(1)} custom-call(f32[1,128,128]{2,1,0:T(8,128)S(1)} %get-tuple-element.124), custom_call_target="InvertDiagBlocksLowerTriangular" | custom-call | tf_op jit(solution)/shard_map/jit(cholesky)/cholesky | solution.py:70
  269.2 11.7 %cholesky.385 = f32[128,128]{1,0:T(8,128)S(1)} custom-call(f32[128,128]{1,0:T(8,128)S(1)} %cholesky.901), custom_call_target="Cholesky" | custom-call | tf_op jit(solution)/shard_map/jit(cholesky)/cholesky | solution.py:70
  281.5 10.2 %custom-call.97 = f32[1,128,128]{1,2,0:T(8,128)S(1)} custom-call(f32[1,128,128]{2,1,0:T(8,128)S(1)} %get-tuple-element.121), custom_call_target="InvertDiagBlocksLowerTriangular" | custom-call | tf_op jit(solution)/shard_map/jit(cholesky)/cholesky | solution.py:70
  296.7 11.7 %cholesky.715 = f32[128,128]{1,0:T(8,128)S(1)} custom-call(f32[128,128]{1,0:T(8,128)S(1)} %cholesky.906), custom_call_target="Cholesky" | custom-call | tf_op jit(solution)/shard_map/jit(cholesky)/cholesky | solution.py:70
  309.1 9.8 %custom-call.98 = f32[1,128,128]{1,2,0:T(8,128)S(1)} custom-call(f32[1,128,128]{2,1,0:T(8,128)S(1)} %get-tuple-element.118), custom_call_target="InvertDiagBlocksLowerTriangular" | custom-call | tf_op jit(solution)/shard_map/jit(cholesky)/cholesky | solution.py:70
  320.3 3.6 slice_subtract_fusion.3
  323.9 11.9 %cholesky.734 = f32[128,128]{1,0:T(8,128)S(1)} custom-call(f32[128,128]{1,0:T(8,128)S(1)} %cholesky.911), custom_call_target="Cholesky" | custom-call | tf_op jit(solution)/shard_map/jit(cholesky)/cholesky | solution.py:70
  336.4 9.8 %custom-call.99 = f32[1,128,128]{1,2,0:T(8,128)S(1)} custom-call(f32[1,128,128]{2,1,0:T(8,128)S(1)} %get-tuple-element.115), custom_call_target="InvertDiagBlocksLowerTriangular" | custom-call | tf_op jit(solution)/shard_map/jit(cholesky)/cholesky | solution.py:70
  347.6 3.9 slice_subtract_fusion.4
  351.5 11.7 %cholesky.754 = f32[128,128]{1,0:T(8,128)S(1)} custom-call(f32[128,128]{1,0:T(8,128)S(1)} %cholesky.916), custom_call_target="Cholesky" | custom-call | tf_op jit(solution)/shard_map/jit(cholesky)/cholesky | solution.py:70
  363.9 10.0 %custom-call.100 = f32[1,128,128]{1,2,0:T(8,128)S(1)} custom-call(f32[1,128,128]{2,1,0:T(8,128)S(1)} %get-tuple-element.112), custom_call_target="InvertDiagBlocksLowerTriangular" | custom-call | tf_op jit(solution)/shard_map/jit(cholesky)/cholesky | solution.py:70
  375.1 3.8 slice_subtract_fusion.5
  379.0 11.7 %cholesky.774 = f32[128,128]{1,0:T(8,128)S(1)} custom-call(f32[128,128]{1,0:T(8,128)S(1)} %cholesky.921), custom_call_target="Cholesky" | custom-call | tf_op jit(solution)/shard_map/jit(cholesky)/cholesky | solution.py:70
  391.3 9.8 %custom-call.101 = f32[1,128,128]{1,2,0:T(8,128)S(1)} custom-call(f32[1,128,128]{2,1,0:T(8,128)S(1)} %get-tuple-element.109), custom_call_target="InvertDiagBlocksLowerTriangular" | custom-call | tf_op jit(solution)/shard_map/jit(cholesky)/cholesky | solution.py:70
  402.3 4.3 slice_subtract_fusion.6
  406.6 11.7 %cholesky.794 = f32[128,128]{1,0:T(8,128)S(1)} custom-call(f32[128,128]{1,0:T(8,128)S(1)} %cholesky.926), custom_call_target="Cholesky" | custom-call | tf_op jit(solution)/shard_map/jit(cholesky)/cholesky | solution.py:70
  419.0 9.8 %custom-call.102 = f32[1,128,128]{1,2,0:T(8,128)S(1)} custom-call(f32[1,128,128]{2,1,0:T(8,128)S(1)} %get-tuple-element.106), custom_call_target="InvertDiagBlocksLowerTriangular" | custom-call | tf_op jit(solution)/shard_map/jit(cholesky)/cholesky | solution.py:70
  429.9 3.6 slice_subtract_fusion.7
  433.5 11.8 %cholesky.814 = f32[128,128]{1,0:T(8,128)S(1)} custom-call(f32[128,128]{1,0:T(8,128)S(1)} %cholesky.931), custom_call_target="Cholesky" | custom-call | tf_op jit(solution)/shard_map/jit(cholesky)/cholesky | solution.py:70
  445.9 9.8 %custom-call.103 = f32[1,128,128]{1,2,0:T(8,128)S(1)} custom-call(f32[1,128,128]{2,1,0:T(8,128)S(1)} %get-tuple-element.103), custom_call_target="InvertDiagBlocksLowerTriangular" | custom-call | tf_op jit(solution)/shard_map/jit(cholesky)/cholesky | solution.py:70
  460.1 11.7 %cholesky.834 = f32[128,128]{1,0:T(8,128)S(1)} custom-call(f32[128,128]{1,0:T(8,128)S(1)} %cholesky.936), custom_call_target="Cholesky" | custom-call | tf_op jit(solution)/shard_map/jit(cholesky)/cholesky | solution.py:70
  472.4 9.8 %custom-call.104 = f32[1,128,128]{1,2,0:T(8,128)S(1)} custom-call(f32[1,128,128]{2,1,0:T(8,128)S(1)} %get-tuple-element.100), custom_call_target="InvertDiagBlocksLowerTriangular" | custom-call | tf_op jit(solution)/shard_map/jit(cholesky)/cholesky | solution.py:70
  485.9 12.1 %cholesky.854 = f32[128,128]{1,0:T(8,128)S(1)} custom-call(f32[128,128]{1,0:T(8,128)S(1)} %cholesky.941), custom_call_target="Cholesky" | custom-call | tf_op jit(solution)/shard_map/jit(cholesky)/cholesky | solution.py:70
  498.7 9.8 %custom-call.105 = f32[1,128,128]{1,2,0:T(8,128)S(1)} custom-call(f32[1,128,128]{2,1,0:T(8,128)S(1)} %get-tuple-element.97), custom_call_target="InvertDiagBlocksLowerTriangular" | custom-call | tf_op jit(solution)/shard_map/jit(cholesky)/cholesky | solution.py:70
  511.6 11.7 %cholesky.872 = f32[128,128]{1,0:T(8,128)S(1)} custom-call(f32[128,128]{1,0:T(8,128)S(1)} %slice_subtract_fusion.10), custom_call_target="Cholesky" | custom-call | tf_op jit(solution)/shard_map/jit(cholesky)/cholesky | solution.py:70
  538.7 12.9 %fusion.1 = (f32[1536,1536]{1,0:T(8,128)}, f32[1536,1536]{1,0:T(8,128)}) fusion(f32[1536,1536]{1,0:T(8,128)} %get-tuple-element.95, pred[]{:T(512)S(6)} %cholesky.891), kind=kLoop, calls=%fused_computation.8 | loop fusion | flops 9437184 | bytes 28311552 | tf_op jit(solution)/shard_map/jit(_solve_triangular)/triangular_solve | solution.py:86
  551.7 42.0 %while.1 = (s32[]{:T(128)}, f32[1536,1536]{1,0:T(8,128)}, s32[12,2]{0,1:T(2,128)S(1)}, f32[12,128,128]{2,1,0:T(8,128)}, s32[]{:T(128)}) while((s32[]{:T(128)}, f32[1536,1536]{1,0:T(8,128)}, s32[12,2]{0,1:T(2,128)S(1)}, f32[12,128,128]{2,1,0:T(8,128)}, s32[]{:T(128)}) %tuple.110), condition=%wide.while_cond, body=%wide.while_body.sunk | while | flops 2 | bytes 132205 | solution.py:86
  593.7 118.7 %custom-call.106 = f32[12,128,128]{1,2,0:T(8,128)S(1)} custom-call(f32[12,128,128]{2,1,0:T(8,128)} %get-tuple-element.10), custom_call_target="InvertDiagBlocksLowerTriangular" | custom-call | tf_op jit(solution)/shard_map/jit(_solve_triangular)/triangular_solve | solution.py:86
  712.4 16.9 %copy.32 = bf16[2,1536,8,256]{3,2,0,1:T(8,128)(2,1)} copy(bf16[2,1536,8,256]{1,3,2,0:T(8,128)(2,1)} %bitcast.191) | data formatting | bytes 25165824 | tf_op jit(solution)/shard_map/reshape | solution.py:82
  729.3 9.2 %fusion.130 = f32[1536,256,4,1]{1,2,3,0:T(4,128)} fusion(bf16[2,1536,8,256]{3,2,0,1:T(8,128)(2,1)} %copy.32, s32[2,8]{1,0:T(2,128)S(1)} %gather_fusion, s32[4]{0:T(128)S(1)} %iota_add_fusion), kind=kOutput, calls=%fused_computation.259 | convolution fusion | flops 50331712 | bytes 18874448 | tf_op jit(solution)/shard_map/cno,cfnb->fob/dot_general | solution.py:84
  738.6 4.5 copy.33
  772.1 4.1 convolution_subtract_fusion.5
  776.9 4.1 convolution_subtract_fusion.3
  781.6 4.5 convolution_subtract_fusion.8
  790.5 29.2 %all-reduce.3.cloned.1.call-done = bf16[1536,256]{1,0:T(8,128)(2,1)} async-done(((bf16[1536,256]{1,0:T(8,128)(2,1)}), bf16[1536,256]{1,0:T(8,128)(2,1)}) %all-reduce.3.cloned.1.call-update) | async-done | bytes 786448 | tf_op jit(solution)/shard_map/psum | solution.py:18
  824.5 14.5 %collective-permute-done.3 = bf16[1536,256]{1,0:T(8,128)(2,1)S(1)} collective-permute-done((bf16[1536,256]{1,0:T(8,128)(2,1)}, bf16[1536,256]{1,0:T(8,128)(2,1)S(1)}, u32[]{:S(2)}, u32[]{:S(2)}) %collective-permute-start.3) | collective-permute-done | bytes 786464 | tf_op jit(solution)/shard_map/ppermute | solution.py:13
  840.4 11.4 %fusion.24 = f32[1,512,1024]{2,1,0:T(8,128)} fusion(f32[1536,1024]{1,0:T(8,128)S(1)} %copy-done.3, f32[1536,256]{1,0:T(8,128)S(1)} %get-tuple-element.26, f32[1536,256]{1,0:T(8,128)S(1)} %get-tuple-element.25, bf16[1,512,1024]{2,1,0:T(8,128)(2,1)S(1)} %copy-done.7), kind=kOutput, calls=%fused_computation.38 | convolution fusion | flops 9665511424 | bytes 12582912 | tf_op jit(solution)/shard_map/dot_general | solution.py:98
  (166 shorter events, 150.8 us)
Async XLA Ops:
  7.2 92.2 %copy-start = (s32[64,8]{0,1:T(8,128)S(1)}, s32[64,8]{0,1:T(8,128)}, u32[]{:S(2)}) copy-start(s32[64,8]{0,1:T(8,128)} %param.10) | copy-start | bytes 6148
  7.2 33.2 %copy-start.5 = (bf16[1,768,1536]{2,1,0:T(8,128)(2,1)S(1)}, bf16[1,768,1536]{2,1,0:T(8,128)(2,1)}, u32[]{:S(2)}) copy-start(bf16[1,768,1536]{2,1,0:T(8,128)(2,1)} %param.12) | copy-start | bytes 7077892
  7.2 167.2 %all-gather.10.cloned.1.call-start = ((), (), s32[]{:S(2)}) async-start(), calls=%async_computation.2 | async-start | bytes 3538944 | tf_op jit(solution)/shard_map/all_gather | solution.py:65
  9.1 27.4 %collective-permute-start.1 = (bf16[1,384,1536]{1,2,0:T(8,128)(2,1)S(1)}, bf16[1,384,1536]{1,2,0:T(8,128)(2,1)}, u32[]{:S(2)}, u32[]{:S(2)}) collective-permute-start(bf16[1,384,1536]{1,2,0:T(8,128)(2,1)S(1)} %copy.24), channel_id=1, source_target_pairs={{0,2},{2,0},{4,6},{6,4},{8,10},{10,8},{12,14},{14,12},{16,18},{18,... | collective-permute-start | bytes 3538952 | tf_op jit(solution)/shard_map/ppermute | solution.py:13
  39.6 134.9 %all-gather.12.cloned.1.call-start = ((), (), s32[]{:S(2)}) async-start(), calls=%async_computation.3 | async-start | bytes 3538944 | tf_op jit(solution)/shard_map/all_gather | solution.py:66
  40.3 134.1 %all-gather.6.cloned.1.call-start = ((), (), s32[]{:S(2)}) async-start(), calls=%async_computation | async-start | bytes 7077888 | tf_op jit(solution)/shard_map/all_gather | solution.py:63
  42.8 60.6 %copy-start.8 = (s32[64,8]{0,1:T(8,128)S(1)}, s32[64,8]{0,1:T(8,128)}, u32[]{:S(2)}) copy-start(s32[64,8]{0,1:T(8,128)} %param.11) | copy-start | bytes 6148
  42.8 131.6 %all-gather.8.cloned.1.call-start = ((), (), s32[]{:S(2)}) async-start(), calls=%async_computation.1 | async-start | bytes 7077888 | tf_op jit(solution)/shard_map/all_gather | solution.py:64
  42.9 51.7 %collective-permute-start = (bf16[1,768,1536]{1,2,0:T(8,128)(2,1)}, bf16[1,768,1536]{1,2,0:T(8,128)(2,1)S(1)}, u32[]{:S(2)}, u32[]{:S(2)}) collective-permute-start(bf16[1,768,1536]{1,2,0:T(8,128)(2,1)} %copy.21), channel_id=1, source_target_pairs={{0,2},{2,0},{4,6},{6,4},{8,10},{10,8},{12,14},{14,12},{16,18},{18,... | collective-permute-start | bytes 7077896 | tf_op jit(solution)/shard_map/ppermute | solution.py:13
  94.5 1.4 copy-start.6
  96.0 616.4 %all-gather.14.cloned.1.call-start = ((), (), s32[]{:S(2)}) async-start(), calls=%async_computation.4 | async-start | bytes 18874368 | tf_op jit(solution)/shard_map/all_gather | solution.py:80
  101.8 67.3 %collective-permute-start.2 = (bf16[1536,1024]{0,1:T(8,128)(2,1)S(1)}, bf16[1536,1024]{0,1:T(8,128)(2,1)}, u32[]{:S(2)}, u32[]{:S(2)}) collective-permute-start(bf16[1536,1024]{0,1:T(8,128)(2,1)S(1)} %bitcast.192), channel_id=1, source_target_pairs={{0,2},{2,0},{4,6},{6,4},{8,10},{10,8},{12,14},{14,12},{16,18},{18,... | collective-permute-start | bytes 9437192 | tf_op jit(solution)/shard_map/ppermute | solution.py:13
  174.3 645.4 %all-reduce.3.cloned.1.call-start = ((), (), s32[]{:S(2)}) async-start(), calls=%async_computation.5 | async-start | bytes 1572864 | tf_op jit(solution)/shard_map/psum | solution.py:18
  738.6 4.5 copy-start.4
  786.8 2.7 copy-start.2
  789.5 50.9 %copy-start.7 = (bf16[1,512,1024]{2,1,0:T(8,128)(2,1)S(1)}, bf16[1,512,1024]{2,1,0:T(8,128)(2,1)}, u32[]{:S(2)}) copy-start(bf16[1,512,1024]{2,1,0:T(8,128)(2,1)} %param.15) | copy-start | bytes 3145732
  819.7 19.3 %collective-permute-start.3 = (bf16[1536,256]{1,0:T(8,128)(2,1)}, bf16[1536,256]{1,0:T(8,128)(2,1)S(1)}, u32[]{:S(2)}, u32[]{:S(2)}) collective-permute-start(bf16[1536,256]{1,0:T(8,128)(2,1)} %all-reduce.3.cloned.1.call-done), channel_id=1, source_target_pairs={{0,2},{2,0},{4,6},{6,4},{8,10},{10,8},{12,14},{14,12},{16,18},{18,... | collective-permute-start | bytes 2359304 | tf_op jit(solution)/shard_map/ppermute | solution.py:13
  821.2 19.2 %copy-start.3 = (f32[1536,1024]{1,0:T(8,128)S(1)}, f32[1536,1024]{1,0:T(8,128)}, u32[]{:S(2)}) copy-start(f32[1536,1024]{1,0:T(8,128)} %copy-done.2) | copy-start | bytes 18874372
  840.4 11.4 %copy-start.1 = (s32[64,8]{0,1:T(8,128)S(1)}, s32[64,8]{0,1:T(8,128)}, u32[]{:S(2)}) copy-start(s32[64,8]{0,1:T(8,128)} %param.10) | copy-start | bytes 6148
Sparse Core Ops, SparseCore 0:
  39.7 17.7 all-gather.9
  59.1 14.9 all-gather.11
  76.3 18.4 all-gather.5
  96.3 21.8 all-gather.7
  174.4 32.8 all-gather.13
  790.6 28.9 all-reduce.2
where the time goes:
time: 866 us; the launch traced here: 859 us
  other arithmetic  433 us (50%)
  waiting for transfers between devices  185 us (21%)
  matrix products  115 us (13%)
  local copies, waits for them, and re-layouts  95.7 us (11%)
  between operations  22.8 us (3%)
    another operation x46, other arithmetic, shards(): factor = jnp.linalg.cholesky(lead)  264 us
    ppermute x4, waiting for transfers between devices, partner_2(): return lax.ppermute(value, axis, pairs)  155 us
    another operation x3, other arithmetic, shards(): upper = jax.scipy.linalg.solve_triangular(factor, assembled, lower=True)  132 us
    another operation x22, matrix products, shards(): factor = jnp.linalg.cholesky(lead)  50.4 us
    another operation x36, local copies, waits for them, and re-layouts  42 us
    another operation x23, matrix products, shards(): upper = jax.scipy.linalg.solve_triangular(factor, assembled, lower=True)  41.9 us
    psum x1, waiting for transfers between devices, spread_2(): return lax.psum(block, axis)  29.2 us
  transfers between devices with their start and end apart: 10, of which 5 were waited for; matrix products, arithmetic and copies ran while one was open for 64% of the time, Pallas kernels for 0%

commit v1 on v0

v1 whole, which is shorter than its diff:
```python
import functools

import jax
import jax.numpy as jnp
from jax import lax
from jax.experimental import pallas as pl
from jax.experimental.pallas import tpu as pltpu
from jax.sharding import PartitionSpec as P

MESH = pl.DeviceIdType.MESH
F32 = jnp.float32
BF16 = jnp.bfloat16
N = 1536
NB = 256
H = 128
STEPS = N // NB
HALF = N // 2
QUARTER = N // 4
RMAX = 64


def split(x):
    hi = x.astype(BF16)
    return hi, (x - hi.astype(F32)).astype(BF16)


def dot(a, b):
    return jnp.dot(a, b, preferred_element_type=F32)


def dot3(ah, al, bh, bl):
    return dot(ah, bh) + (dot(ah, bl) + dot(al, bh))


def dot_split(a, b):
    return dot3(*split(a), *split(b))


def factor_128(r_ref, x_ref, u_out, x_out):
    sub = lax.broadcasted_iota(jnp.int32, (8, H), 0)

    def panel(p, carry):
        top, rest = r_ref[0:8, :], r_ref[8:H, :]
        xtop, xrest = x_ref[0:8, :], x_ref[8:H, :]
        scale = jnp.ones((8, H), F32)
        for i in range(8):
            ctop = jnp.broadcast_to(top[:, i : i + 1], (8, H))
            crest = jnp.broadcast_to(rest[:, i : i + 1], (H - 8, H))
            pivot = ctop[i : i + 1, :]
            inv = 1.0 / pivot
            row = top[i : i + 1, :] * inv
            xrow = xtop[i : i + 1, :] * inv
            ctop = jnp.where(sub > i, ctop, 0.0)
            scale = jnp.where(sub == i, pivot, scale)
            top = top - ctop * row
            xtop = xtop - ctop * xrow
            rest = rest - crest * row
            xrest = xrest - crest * xrow
        scale = lax.rsqrt(scale)
        rows = pl.ds(pl.multiple_of(p * 8, 8), 8)
        u_out[rows, :] = pltpu.roll(top * scale, p * 8, 1)
        x_out[rows, :] = xtop * scale
        r_ref[0 : H - 8, :] = pltpu.roll(rest, H - 8, 1)
        r_ref[H - 8 : H, :] = jnp.zeros((8, H), F32)
        x_ref[0 : H - 8, :] = xrest
        x_ref[H - 8 : H, :] = jnp.zeros((8, H), F32)
        return carry

    lax.fori_loop(0, H // 8, panel, 0)
    low = lax.broadcasted_iota(jnp.int32, (H, H), 0)
    col = lax.broadcasted_iota(jnp.int32, (H, H), 1)
    u_out[...] = jnp.where(col >= low, u_out[...], 0.0)


def eye():
    low = lax.broadcasted_iota(jnp.int32, (H, H), 0)
    col = lax.broadcasted_iota(jnp.int32, (H, H), 1)
    return jnp.where(col == low, 1.0, 0.0).astype(F32)


def cols(j):
    return pl.ds(pl.multiple_of(j * NB, NB), NB)


def factor_kernel(
    child, orig, fl, fr, op,
    out_lead, lh, ll, xh, xl, flg, frg, opg,
    ca, cb, og, ox, apan, lf, uh, ul, xf, r_ref, w_ref, u_a, x_a, u_b, x_b,
    loc, sib_send, sib_recv, x_send, relay_send, x_recv, out_sem,
):
    leaf, core = lax.axis_index("leaf"), lax.axis_index("front")
    par = lax.rem(leaf, 2)
    sibling = (leaf, 1 - core)
    xpeer = (leaf + 1 - 2 * par, core)
    barrier = pltpu.get_barrier_semaphore()
    for other in (sibling, xpeer):
        pl.semaphore_signal(barrier, inc=1, device_id=other, device_id_type=MESH)
    pl.semaphore_wait(barrier, 2)

    def slot(ref, index, width):
        return ref.at[:, pl.ds(pl.multiple_of(index * width, 128), width)]

    own = []
    for k in range(STEPS):
        own.append((k // 3, child.at[pl.ds(k % 3 * NB, NB), pl.ds(k * NB, N - k * NB)],
                    ca.at[pl.ds(k * NB, NB), pl.ds(k * NB, N - k * NB)]))
    for c in range(2):
        own.append((c, orig, og.at[pl.ds(c * QUARTER, QUARTER), :]))
    for c in range(2):
        own.append((c, fl, slot(flg, 2 * par + c, 256)))
    for c in range(2):
        own.append((c, fr, slot(frg, 2 * par + c, 256)))
    own.append((0, op.at[:, pl.ds(0, NB)], slot(opg, par, NB)))

    cross = []
    for k in range(STEPS):
        there = cb.at[pl.ds(k * NB, NB), pl.ds(k * NB, N - k * NB)]
        cross.append((k // 3, own[k][1], there, there))
    for g in range(6):
        start = g * H
        width = HALF - start
        src = orig.at[pl.ds(g % 3 * H, H), pl.ds(pl.multiple_of(par * HALF + start, 128), width)]
        there = ox.at[pl.ds(start, H), pl.ds(start, width)]
        cross.append((g // 3, src, there, there))
    for c in range(2):
        cross.append((c, fl, slot(flg, 2 * par + c, 256), slot(flg, 2 * (1 - par) + c, 256)))
    for c in range(2):
        cross.append((c, fr, slot(frg, 2 * par + c, 256), slot(frg, 2 * (1 - par) + c, 256)))
    cross.append((0, op.at[:, pl.ds(0, NB)], slot(opg, par, NB), slot(opg, 1 - par, NB)))

    def local(n):
        return pltpu.make_async_copy(own[n][1], own[n][2], loc.at[n])

    def to_sibling(n):
        return pltpu.make_async_remote_copy(own[n][1], own[n][2], sib_send.at[n], sib_recv.at[n],
                                            device_id=sibling, device_id_type=MESH)

    def to_peer(n):
        return pltpu.make_async_remote_copy(cross[n][1], cross[n][2], x_send.at[n], x_recv.at[n],
                                            device_id=xpeer, device_id_type=MESH)

    def relay(n):
        return pltpu.make_async_remote_copy(cross[n][3], cross[n][3], relay_send.at[n], x_recv.at[n],
                                            device_id=sibling, device_id_type=MESH)

    def start_own(n):
        @pl.when(core == own[n][0])
        def _():
            local(n).start()
            to_sibling(n).start()

    def wait_own(n):
        @pl.when(core == own[n][0])
        def _():
            local(n).wait()

        @pl.when(core != own[n][0])
        def _():
            to_sibling(n).wait_recv()

    def start_cross(n):
        @pl.when(core == cross[n][0])
        def _():
            to_peer(n).start()

    def take_cross(n):
        relay(n).wait_recv()

        @pl.when(core == cross[n][0])
        def _():
            relay(n).start()

    fac = (8, 9, 10, 11, 12)
    xfac = (12, 13, 14, 15, 16)
    for n in (0, 6, 7):
        start_own(n)
    for n in (0, 6, 7):
        start_cross(n)
    for n in (1, 2, 3, 4, 5):
        start_own(n)
    for n in (1, 8, 2):
        start_cross(n)
    for k in range(STEPS):
        lf[pl.ds(k * NB, NB), :] = jnp.zeros((NB, N), F32)

    for k in range(STEPS):
        rows = slice(k * NB, (k + 1) * NB)
        wait_own(k)
        if k == 0:
            wait_own(6)
            wait_own(7)
        take_cross(k)
        if k < 3:
            take_cross(6 + 2 * k)
            take_cross(7 + 2 * k)
        if k == 0:
            for n in (9, 10, 11, 3, 4, 5):
                start_cross(n)
            for n in fac:
                start_own(n)
        if k == 1:
            for n in xfac:
                start_cross(n)

        def assemble(lo, hi, piece):
            @pl.loop(lo, hi)
            def _(j):
                both = ca[rows, cols(j)].astype(F32) + cb[rows, cols(j)].astype(F32)
                apan[:, cols(j)] = both + piece(j)

        if k < 3:
            @pl.when(par == 0)
            def _():
                assemble(k, STEPS, lambda j: og[rows, cols(j)].astype(F32))

            @pl.when(par == 1)
            def _():
                assemble(k, 3, lambda j: ox[rows, cols(j)].astype(F32))
                assemble(3, STEPS, lambda j: og[cols(j - 3), rows].astype(F32).T)
        else:
            part = slice(rows.start - HALF, rows.stop - HALF)

            @pl.when(par == 0)
            def _():
                assemble(k, STEPS, lambda j: ox[part, cols(j - 3)].astype(F32))

            @pl.when(par == 1)
            def _():
                assemble(k, STEPS, lambda j: og[part, cols(j)].astype(F32))

        def updated(j):
            block = apan[:, cols(j)]
            if k == 0:
                return block
            done = slice(0, k * NB)
            return block - dot3(lh[rows, done], ll[rows, done], uh[done, cols(j)], ul[done, cols(j)])

        diag = updated(k)
        r_ref[...] = diag[:H, :H]
        w_ref[...] = eye()
        apan[:, rows] = diag
        factor_128(r_ref, w_ref, u_a, x_a)
        xa = x_a[...]
        uab = dot_split(xa, apan[0:H, rows.start + H : rows.stop])
        lba = uab.T
        r_ref[...] = apan[H:NB, rows.start + H : rows.stop] - dot_split(lba, uab)
        w_ref[...] = eye()
        factor_128(r_ref, w_ref, u_b, x_b)
        xf[0:H, 0:H] = xa
        xf[0:H, H:NB] = jnp.zeros((H, H), F32)
        xf[H:NB, 0:H] = -dot_split(x_b[...], dot_split(lba, xa))
        xf[H:NB, H:NB] = x_b[...]
        mid = rows.start + H
        lf[rows.start : mid, rows.start : mid] = u_a[...].T
        lf[mid : rows.stop, rows.start : mid] = lba
        lf[mid : rows.stop, mid : rows.stop] = u_b[...].T
        hi, lo = split(xf[...])
        xh[rows, :] = hi
        xl[rows, :] = lo
        if k < STEPS - 1:
            @pl.loop(k + 1, STEPS)
            def _(j):
                bh, bl = split(updated(j))
                u = dot3(xh[rows, :], xl[rows, :], bh, bl)
                uhi, ulo = split(u)
                uh[rows, cols(j)] = uhi
                ul[rows, cols(j)] = ulo
                t = u.T
                lf[cols(j), rows] = t
                thi, tlo = split(t)
                lh[cols(j), rows] = thi
                ll[cols(j), rows] = tlo

    mine = pl.ds(pl.multiple_of(par * HALF + core * QUARTER, 128), QUARTER)
    write = pltpu.make_async_copy(lf.at[mine, :], out_lead, out_sem)
    write.start()
    for n in xfac:
        take_cross(n)
    for n in fac:
        wait_own(n)
    for n in range(len(own)):
        @pl.when(core == own[n][0])
        def _():
            to_sibling(n).wait_send()
    for n in range(len(cross)):
        @pl.when(core == cross[n][0])
        def _():
            to_peer(n).wait_send()
            relay(n).wait_send()
    write.wait()


def factor_call(child, orig, fl, fr, op):
    any_spec = pl.BlockSpec(memory_space=pl.ANY)
    vmem = pl.BlockSpec(memory_space=pltpu.VMEM)
    dma = pltpu.SemaphoreType.DMA
    return pl.pallas_call(
        factor_kernel,
        out_shape=(
            jax.ShapeDtypeStruct((QUARTER, N), F32),
            jax.ShapeDtypeStruct((N, N), BF16),
            jax.ShapeDtypeStruct((N, N), BF16),
            jax.ShapeDtypeStruct((N, NB), BF16),
            jax.ShapeDtypeStruct((N, NB), BF16),
            jax.ShapeDtypeStruct((N, 1024), BF16),
            jax.ShapeDtypeStruct((NB, 1024), BF16),
            jax.ShapeDtypeStruct((N, 512), BF16),
        ),
        in_specs=[any_spec] * 5,
        out_specs=(any_spec, vmem, vmem, vmem, vmem, any_spec, any_spec, any_spec),
        scratch_shapes=[
            pltpu.VMEM((N, N), BF16),
            pltpu.VMEM((N, N), BF16),
            pltpu.VMEM((HALF, N), BF16),
            pltpu.VMEM((HALF, HALF), BF16),
            pltpu.VMEM((NB, N), F32),
            pltpu.VMEM((N, N), F32),
            pltpu.VMEM((N, N), BF16),
            pltpu.VMEM((N, N), BF16),
            pltpu.VMEM((NB, NB), F32),
        ]
        + [pltpu.VMEM((H, H), F32)] * 6
        + [dma((13,)), dma((13,)), dma((13,)), dma((17,)), dma((17,)), dma((17,)), dma(())],
        compiler_params=pltpu.CompilerParams(
            collective_id=0, has_side_effects=True, vmem_limit_bytes=56 << 20
        ),
        name="factor",
    )(child, orig, fl, fr, op)


def solve_kernel(lh, ll, xh, xl, fl, fr, op, panel, mask, onext, upper, below, rh, rl, wt):
    step = pl.program_id(0)
    width = panel.shape[1]
    right = jnp.concatenate([fr[...] * mask[0, o : o + 1, :] for o in range(width // NB)], axis=0)

    def orig_rows(rows):
        return jnp.where(step == 0, op[rows, :], panel[rows, :]).astype(F32)

    for k in range(STEPS):
        rows = slice(k * NB, (k + 1) * NB)
        acc = orig_rows(rows) + lax.dot_general(
            fl[rows, :], right, (((1,), (1,)), ((), ())), preferred_element_type=F32
        )
        if k > 0:
            done = slice(0, k * NB)
            acc = acc - dot3(lh[rows, done], ll[rows, done], rh[done, :], rl[done, :])
        bh, bl = split(acc)
        u = dot3(xh[rows, :], xl[rows, :], bh, bl)
        uhi, ulo = split(u)
        rh[rows, :] = uhi
        rl[rows, :] = ulo
        upper[rows, :] = u

        @pl.when(step == 0)
        def _():
            wt[:, rows] = u.T.astype(BF16)

    @pl.when(step > 0)
    def _():
        below[...] = onext[...].astype(F32) - dot(wt[...], rh[...])


def solve_call(lh, ll, xh, xl, fl, fr, op, panel, mask, onext):
    width = 512
    count = panel.shape[1] // width

    def whole(x):
        return pl.BlockSpec(x.shape, lambda t: (0, 0), pipeline_mode=pl.Buffered(1))

    def tile(x):
        return pl.BlockSpec((x.shape[0], width), lambda t: (0, jnp.maximum(t - 1, 0)))

    return pl.pallas_call(
        solve_kernel,
        grid=(count + 1,),
        out_shape=(
            jax.ShapeDtypeStruct(panel.shape, F32),
            jax.ShapeDtypeStruct(onext.shape, F32),
        ),
        in_specs=[whole(x) for x in (lh, ll, xh, xl, fl, fr, op)]
        + [tile(panel), pl.BlockSpec((1, 2, 1024), lambda t: (t, 0, 0)), tile(onext)],
        out_specs=(tile(panel), tile(onext)),
        scratch_shapes=[
            pltpu.VMEM((N, width), BF16),
            pltpu.VMEM((N, width), BF16),
            pltpu.VMEM((512, N), BF16),
        ],
        compiler_params=pltpu.CompilerParams(vmem_limit_bytes=56 << 20),
        name="solve",
    )(lh, ll, xh, xl, fl, fr, op, panel, mask, onext)


def shards(fac_left, fac_right, block_rank, col_map, child_lead, orig_lead, orig_panel, orig_next):
    leaf, core = lax.axis_index("leaf"), lax.axis_index("front")
    par = leaf % 2
    out_lead, lh, ll, xh, xl, flg, frg, opg = factor_call(
        child_lead[0], orig_lead[0], fac_left[0], fac_right[0], orig_panel[0]
    )
    own = par * 8 + core * 4 + jnp.arange(4, dtype=jnp.int32)
    targets = jnp.concatenate([jnp.array([0, 8], jnp.int32), own])
    maps = lax.dynamic_slice_in_dim(col_map, leaf - par, 2, 0).reshape(16)
    ranks = lax.dynamic_slice_in_dim(block_rank, leaf - par, 2, 0).reshape(16)
    live = jnp.arange(RMAX)[None, :] < ranks[:, None]
    hit = targets[:, None] == maps[None, :]
    mask = (hit[:, :, None] & live[None]).astype(BF16).reshape(3, 2, 1024)
    upper, below = solve_call(lh, ll, xh, xl, flg, frg, opg, orig_panel[0], mask, orig_next[0])
    return (out_lead[None], upper[None], below[None])


def solution(mesh):
    placed = (
        P("leaf", None, "front"),
        P("leaf", None, "front"),
        P(),
        P(),
        P("leaf", "front", None),
        P("leaf", "front", None),
        P("leaf", None, "front"),
        P("leaf", None, "front"),
    )
    return jax.shard_map(
        shards,
        mesh=mesh,
        in_specs=placed,
        out_specs=(P("leaf", "front", None), P("leaf", None, "front"), P("leaf", None, "front")),
        check_vma=False,
    )
```

time: 866 us -> 243 us (0.28)
  other arithmetic: 433 us -> 0.79 us
  Pallas kernels: 0 us -> 238 us
  waiting for transfers between devices: 185 us -> 0 us
  matrix products: 115 us -> 0 us
  local copies, waits for them, and re-layouts: 95.7 us -> 2.93 us
  between operations: 22.8 us -> 0.71 us
    another operation x50 -> x1, other arithmetic: 401 us -> 0.01 us  [the longest x46 264 us: shards(): factor = jnp.linalg.cholesky(lead)]
    pallas_call x0 -> x2, Pallas kernels: none -> 238 us  [the longest x1 202 us: factor_call(): pl.pallas_call(factor_kernel, out_shape=(jax.ShapeDtypeStruct((QUARTER, N...]
    ppermute x4 -> x0, waiting for transfers between devices: 155 us -> none  [partner_2(): return lax.ppermute(value, axis, pairs)]
    another operation x45 -> x0, matrix products: 92.3 us -> none  [the longest x22 50.4 us: shards(): factor = jnp.linalg.cholesky(lead)]
    another operation x49 -> x0, local copies, waits for them, and re-layouts: 47.7 us -> none
    psum x1 -> x0, waiting for transfers between devices: 29.2 us -> none  [spread_2(): return lax.psum(block, axis)]
    dot_general x3 -> x0, matrix products: 22.8 us -> none  [the longest x1 11.4 us: shards(): jnp.dot(leading.T, upper, precision=lax.Precision.HIGHEST)]
    reshape x1 -> x0, local copies, waits for them, and re-layouts: 16.9 us -> none  [shards(): blocks = piece.reshape(2, order, count, width)]
  transfers between devices with their start and end apart: 10 -> 0, of which waited for: 5 -> 0; matrix products, arithmetic and copies ran while one was open for 64% -> 0% of each run, Pallas kernels for 0% -> 0%
where the time goes in v1:
time: 243 us; the launch traced here: 242 us
  Pallas kernels  238 us (98%)
  local copies, waits for them, and re-layouts  2.93 us (1%)
    pallas_call x1, Pallas kernels, factor_call(): pl.pallas_call(factor_kernel, out_shape=(jax.ShapeDtypeStruct((QUARTER, N...  202 us
    pallas_call x1, Pallas kernels, solve_call(): pl.pallas_call(solve_kernel, grid=(count + 1,), out_shape=(jax.ShapeDtype...  35.6 us

profile of v1, /device:TPU:1, one launch (start us, length us, event | category | flops | bytes accessed | tf_op | source)
XLA Modules:
  0.0 242.4 jit_solution(8897158221812412446)
XLA Ops:
  0.7 0.1 pad_add_fusion
  0.7 0.8 constant_dynamic-slice_fusion
  1.5 0.1 copy.15
  1.6 0.1 lt.37
  1.7 0.1 copy.14
  1.8 0.1 eq.22
  1.9 0.1 broadcast_compare_fusion
  1.9 0.1 broadcast_reduce_fusion
  2.0 0.1 lt.39
  2.1 0.1 lt.36
  2.2 0.1 and.24
  2.3 0.1 and.25
  2.4 0.6 and_convert_fusion.mask
  3.0 202.4 %factor.1 = (f32[384,1536]{1,0:T(8,128)}, bf16[1536,1536]{1,0:T(8,128)(2,1)}, bf16[1536,1536]{1,0:T(8,128)(2,1)}, bf16[1536,256]{1,0:T(8,128)(2,1)}, bf16[1536,2...) custom-call(bf16[768,1536]{1,0:T(8,128)(2,1)} %bitcast.12, ...), custom_call_target="tpu_custom_call" | custom-call | tf_op jit(solution)/shard_map/factor/pallas_call | solution.py:297
  205.4 0.0 copy-start
  205.4 35.6 %solve.1 = (f32[1536,1024]{1,0:T(8,128)}, f32[512,1024]{1,0:T(8,128)}) custom-call(bf16[1536,1536]{1,0:T(8,128)(2,1)} %get-tuple-element.14.lh, bf16[1536,1536]{1,0:T(8,128)(2,1)} %get-tuple-element.15.ll, bf16[1536,256]{1,0:T(8,128)(2,1)} %get-tuple-element.16.xh, bf16[1536,256]{1,0:T(8,128)(2,1)} %get-tuple-element.17.xl, ...), custom_call_target="tpu_custom_call" | custom-call | tf_op jit(solution)/shard_map/solve/pallas_call | solution.py:373
  240.9 0.0 copy-done
  240.9 1.4 copy.17
  (4 shorter events, 0.0 us)
Async XLA Ops:
  205.4 35.6 %copy-start = (f32[384,1536]{1,0:T(8,128)S(1)}, f32[384,1536]{1,0:T(8,128)}, u32[]{:S(2)}) copy-start(f32[384,1536]{1,0:T(8,128)} %get-tuple-element.13) | copy-start | bytes 7077892

commit v2 on v1

--- a/solution.py
+++ b/solution.py
@@ -17,6 +17,7 @@
 HALF = N // 2
 QUARTER = N // 4
 RMAX = 64
+W = 32
 
 
 def split(x):
@@ -37,39 +38,49 @@
 
 
 def factor_128(r_ref, x_ref, u_out, x_out):
-    sub = lax.broadcasted_iota(jnp.int32, (8, H), 0)
+    sub = lax.broadcasted_iota(jnp.int32, (W, H), 0)
 
     def panel(p, carry):
-        top, rest = r_ref[0:8, :], r_ref[8:H, :]
-        xtop, xrest = x_ref[0:8, :], x_ref[8:H, :]
-        scale = jnp.ones((8, H), F32)
-        for i in range(8):
-            ctop = jnp.broadcast_to(top[:, i : i + 1], (8, H))
-            crest = jnp.broadcast_to(rest[:, i : i + 1], (H - 8, H))
-            pivot = ctop[i : i + 1, :]
+        top, xtop = r_ref[0:W, :], x_ref[0:W, :]
+        col = [jnp.broadcast_to(top[k // 8 * 8 :, k : k + 1], (W - k // 8 * 8, H)) for k in range(W)]
+        pivots = jnp.ones((W, H), F32)
+        inverses = jnp.ones((W, H), F32)
+        for i in range(W):
+            base = i // 8 * 8
+            pivot = col[i][i - base : i - base + 1, :]
             inv = 1.0 / pivot
-            row = top[i : i + 1, :] * inv
-            xrow = xtop[i : i + 1, :] * inv
-            ctop = jnp.where(sub > i, ctop, 0.0)
-            scale = jnp.where(sub == i, pivot, scale)
-            top = top - ctop * row
-            xtop = xtop - ctop * xrow
-            rest = rest - crest * row
-            xrest = xrest - crest * xrow
-        scale = lax.rsqrt(scale)
-        rows = pl.ds(pl.multiple_of(p * 8, 8), 8)
-        u_out[rows, :] = pltpu.roll(top * scale, p * 8, 1)
+            m = jnp.where(sub[base:] > i, col[i] * inv, 0.0)
+            pivots = jnp.where(sub == i, pivot, pivots)
+            inverses = jnp.where(sub == i, inv, inverses)
+            for k in range(i + 1, W):
+                low = k // 8 * 8
+                col[k] = col[k] - m[low - base :] * col[i][k - base : k - base + 1, :]
+            row, xrow = top[i : i + 1, :], xtop[i : i + 1, :]
+            ntop, nxtop = top[base:] - m * row, xtop[base:] - m * xrow
+            top = ntop if base == 0 else jnp.concatenate([top[:base], ntop], axis=0)
+            xtop = nxtop if base == 0 else jnp.concatenate([xtop[:base], nxtop], axis=0)
+        scale = lax.rsqrt(pivots)
+        rows = pl.ds(pl.multiple_of(p * W, W), W)
+        u_out[rows, :] = pltpu.roll(top * scale, p * W, 1)
         x_out[rows, :] = xtop * scale
-        r_ref[0 : H - 8, :] = pltpu.roll(rest, H - 8, 1)
-        r_ref[H - 8 : H, :] = jnp.zeros((8, H), F32)
-        x_ref[0 : H - 8, :] = xrest
-        x_ref[H - 8 : H, :] = jnp.zeros((8, H), F32)
+        th, tl = split(top)
+        vh, vl = split(jnp.concatenate([top * inverses, xtop * inverses], axis=1))
+        update = lax.dot_general(
+            jnp.concatenate([th, th, tl], axis=0),
+            jnp.concatenate([vh, vl, vh], axis=0),
+            (((0,), (0,)), ((), ())),
+            preferred_element_type=F32,
+        )
+        r_ref[0 : H - W, :] = pltpu.roll(r_ref[W:H, :] - update[W:, :H], H - W, 1)
+        r_ref[H - W : H, :] = jnp.zeros((W, H), F32)
+        x_ref[0 : H - W, :] = x_ref[W:H, :] - update[W:, H:]
+        x_ref[H - W : H, :] = jnp.zeros((W, H), F32)
         return carry
 
-    lax.fori_loop(0, H // 8, panel, 0)
+    lax.fori_loop(0, H // W, panel, 0)
     low = lax.broadcasted_iota(jnp.int32, (H, H), 0)
-    col = lax.broadcasted_iota(jnp.int32, (H, H), 1)
-    u_out[...] = jnp.where(col >= low, u_out[...], 0.0)
+    right = lax.broadcasted_iota(jnp.int32, (H, H), 1)
+    u_out[...] = jnp.where(right >= low, u_out[...], 0.0)
 
 
 def eye():

time: 243 us -> 141 us (0.58)
  Pallas kernels: 238 us -> 135 us
    pallas_call x1, Pallas kernels: 202 us -> 99.9 us  [factor_call(): pl.pallas_call(factor_kernel, out_shape=(jax.ShapeDtypeStruct((QUARTER, N...]
where the time goes in v2:
time: 141 us; the launch traced here: 140 us
  Pallas kernels  135 us (96%)
  local copies, waits for them, and re-layouts  2.93 us (2%)
    pallas_call x1, Pallas kernels, factor_call(): pl.pallas_call(factor_kernel, out_shape=(jax.ShapeDtypeStruct((QUARTER, N...  99.9 us
    pallas_call x1, Pallas kernels, solve_call(): pl.pallas_call(solve_kernel, grid=(count + 1,), out_shape=(jax.ShapeDtype...  35.6 us

profile of v2, /device:TPU:1, one launch (start us, length us, event | category | flops | bytes accessed | tf_op | source)
XLA Modules:
  0.0 139.9 jit_solution(12182532406609920499)
XLA Ops:
  0.7 0.1 pad_add_fusion
  0.7 0.8 constant_dynamic-slice_fusion
  1.5 0.1 copy.15
  1.6 0.1 lt.37
  1.7 0.1 copy.14
  1.8 0.1 eq.22
  1.9 0.1 broadcast_compare_fusion
  1.9 0.1 broadcast_reduce_fusion
  2.0 0.1 lt.39
  2.1 0.1 lt.36
  2.2 0.1 and.24
  2.3 0.1 and.25
  2.4 0.6 and_convert_fusion.mask
  3.0 99.9 %factor.1 = (f32[384,1536]{1,0:T(8,128)}, bf16[1536,1536]{1,0:T(8,128)(2,1)}, bf16[1536,1536]{1,0:T(8,128)(2,1)}, bf16[1536,256]{1,0:T(8,128)(2,1)}, bf16[1536,2...) custom-call(bf16[768,1536]{1,0:T(8,128)(2,1)} %bitcast.12, ...), custom_call_target="tpu_custom_call" | custom-call | tf_op jit(solution)/shard_map/factor/pallas_call | solution.py:308
  102.9 0.0 copy-start
  102.9 35.6 %solve.1 = (f32[1536,1024]{1,0:T(8,128)}, f32[512,1024]{1,0:T(8,128)}) custom-call(bf16[1536,1536]{1,0:T(8,128)(2,1)} %get-tuple-element.14.lh, bf16[1536,1536]{1,0:T(8,128)(2,1)} %get-tuple-element.15.ll, bf16[1536,256]{1,0:T(8,128)(2,1)} %get-tuple-element.16.xh, bf16[1536,256]{1,0:T(8,128)(2,1)} %get-tuple-element.17.xl, ...), custom_call_target="tpu_custom_call" | custom-call | tf_op jit(solution)/shard_map/solve/pallas_call | solution.py:384
  138.5 0.0 copy-done
  138.5 1.4 %copy.17 = f32[1,384,1536]{2,1,0:T(8,128)} copy(f32[1,384,1536]{2,1,0:T(8,128)S(1)} %bitcast.11) | data formatting | bytes 4718592
  (4 shorter events, 0.0 us)
Async XLA Ops:
  102.9 35.6 %copy-start = (f32[384,1536]{1,0:T(8,128)S(1)}, f32[384,1536]{1,0:T(8,128)}, u32[]{:S(2)}) copy-start(f32[384,1536]{1,0:T(8,128)} %get-tuple-element.13) | copy-start | bytes 7077892

commit v3 on v2

--- a/solution.py
+++ b/solution.py
@@ -95,8 +95,8 @@
 
 def factor_kernel(
     child, orig, fl, fr, op,
-    out_lead, lh, ll, xh, xl, flg, frg, opg,
-    ca, cb, og, ox, apan, lf, uh, ul, xf, r_ref, w_ref, u_a, x_a, u_b, x_b,
+    out_lead, lh_out, ll_out, xh, xl, flg, frg, opg,
+    ca, cb, og, ox, apan, lf, lh, ll, uh, ul, xf, r_ref, w_ref, u_a, x_a, u_b, x_b,
     loc, sib_send, sib_recv, x_send, relay_send, x_recv, out_sem,
 ):
     leaf, core = lax.axis_index("leaf"), lax.axis_index("front")
@@ -111,28 +111,49 @@
     def slot(ref, index, width):
         return ref.at[:, pl.ds(pl.multiple_of(index * width, 128), width)]
 
-    own = []
-    for k in range(STEPS):
-        own.append((k // 3, child.at[pl.ds(k % 3 * NB, NB), pl.ds(k * NB, N - k * NB)],
-                    ca.at[pl.ds(k * NB, NB), pl.ds(k * NB, N - k * NB)]))
-    for c in range(2):
-        own.append((c, orig, og.at[pl.ds(c * QUARTER, QUARTER), :]))
+    def box(ref, row, height, col, width):
+        return ref.at[pl.ds(row, height), pl.ds(col, width)]
+
+    own = [
+        (0, box(child, 0, NB, 0, NB), box(ca, 0, NB, 0, NB)),
+        (0, box(orig, 0, NB, 0, NB), box(og, 0, NB, 0, NB)),
+        (0, box(child, 0, NB, NB, N - NB), box(ca, 0, NB, NB, N - NB)),
+        (0, box(orig, 0, NB, NB, N - NB), box(og, 0, NB, NB, N - NB)),
+        (0, box(orig, NB, H, 0, N), box(og, NB, H, 0, N)),
+        (1, orig, box(og, QUARTER, QUARTER, 0, N)),
+    ]
+    for k in range(1, STEPS):
+        own.append((k // 3, box(child, k % 3 * NB, NB, k * NB, N - k * NB), box(ca, k * NB, NB, k * NB, N - k * NB)))
     for c in range(2):
         own.append((c, fl, slot(flg, 2 * par + c, 256)))
     for c in range(2):
         own.append((c, fr, slot(frg, 2 * par + c, 256)))
     own.append((0, op.at[:, pl.ds(0, NB)], slot(opg, par, NB)))
 
-    cross = []
-    for k in range(STEPS):
-        there = cb.at[pl.ds(k * NB, NB), pl.ds(k * NB, N - k * NB)]
-        cross.append((k // 3, own[k][1], there, there))
-    for g in range(6):
-        start = g * H
-        width = HALF - start
-        src = orig.at[pl.ds(g % 3 * H, H), pl.ds(pl.multiple_of(par * HALF + start, 128), width)]
-        there = ox.at[pl.ds(start, H), pl.ds(start, width)]
-        cross.append((g // 3, src, there, there))
+    def square(c, row, height, start, width):
+        src = box(orig, row, height, pl.multiple_of(par * HALF + start, 128), width)
+        there = box(ox, c * QUARTER + row, height, start, width)
+        return (c, src, there, there)
+
+    def lead_item(k, start, width):
+        src = box(child, k % 3 * NB, NB, start, width)
+        there = box(cb, k * NB, NB, start, width)
+        return (k // 3, src, there, there)
+
+    cross = [
+        lead_item(0, 0, NB),
+        square(0, 0, NB, 0, NB),
+        lead_item(0, NB, N - NB),
+        square(0, 0, NB, NB, HALF - NB),
+        lead_item(1, NB, N - NB),
+        square(0, NB, H, NB, HALF - NB),
+        square(1, 0, H, QUARTER, QUARTER),
+        lead_item(2, 2 * NB, N - 2 * NB),
+        square(1, H, H, QUARTER + H, QUARTER - H),
+        square(1, 2 * H, H, QUARTER + 2 * H, H),
+    ]
+    for k in range(3, STEPS):
+        cross.append(lead_item(k, k * NB, N - k * NB))
     for c in range(2):
         cross.append((c, fl, slot(flg, 2 * par + c, 256), slot(flg, 2 * (1 - par) + c, 256)))
     for c in range(2):
@@ -154,64 +175,57 @@
         return pltpu.make_async_remote_copy(cross[n][3], cross[n][3], relay_send.at[n], x_recv.at[n],
                                             device_id=sibling, device_id_type=MESH)
 
-    def start_own(n):
-        @pl.when(core == own[n][0])
-        def _():
-            local(n).start()
-            to_sibling(n).start()
-
-    def wait_own(n):
-        @pl.when(core == own[n][0])
-        def _():
-            local(n).wait()
-
-        @pl.when(core != own[n][0])
-        def _():
-            to_sibling(n).wait_recv()
-
-    def start_cross(n):
-        @pl.when(core == cross[n][0])
-        def _():
-            to_peer(n).start()
-
-    def take_cross(n):
-        relay(n).wait_recv()
-
-        @pl.when(core == cross[n][0])
-        def _():
-            relay(n).start()
-
-    fac = (8, 9, 10, 11, 12)
-    xfac = (12, 13, 14, 15, 16)
-    for n in (0, 6, 7):
-        start_own(n)
-    for n in (0, 6, 7):
-        start_cross(n)
-    for n in (1, 2, 3, 4, 5):
-        start_own(n)
-    for n in (1, 8, 2):
-        start_cross(n)
+    def start_own(*items):
+        for n in items:
+            @pl.when(core == own[n][0])
+            def _():
+                local(n).start()
+                to_sibling(n).start()
+
+    def wait_own(*items):
+        for n in items:
+            @pl.when(core == own[n][0])
+            def _():
+                local(n).wait()
+
+            @pl.when(core != own[n][0])
+            def _():
+                to_sibling(n).wait_recv()
+
+    def start_cross(*items):
+        for n in items:
+            @pl.when(core == cross[n][0])
+            def _():
+                to_peer(n).start()
+
+    def take_cross(*items):
+        for n in items:
+            relay(n).wait_recv()
+
+            @pl.when(core == cross[n][0])
+            def _():
+                relay(n).start()
+
+    start_cross(0, 1)
+    start_own(0, 1, 2, 3, 4, 5)
     for k in range(STEPS):
         lf[pl.ds(k * NB, NB), :] = jnp.zeros((NB, N), F32)
-
+    wait_own(0, 1)
+    take_cross(0, 1)
+    start_cross(2, 3)
+    start_own(6, 7, 8, 9, 10)
+
+    arrivals = {1: (4, 5, 6), 2: (7, 8, 9), 3: (10,), 4: (11,), 5: (12,)}
+    writes = []
     for k in range(STEPS):
         rows = slice(k * NB, (k + 1) * NB)
-        wait_own(k)
-        if k == 0:
-            wait_own(6)
-            wait_own(7)
-        take_cross(k)
-        if k < 3:
-            take_cross(6 + 2 * k)
-            take_cross(7 + 2 * k)
-        if k == 0:
-            for n in (9, 10, 11, 3, 4, 5):
-                start_cross(n)
-            for n in fac:
-                start_own(n)
+        if k > 0:
+            wait_own(5 + k)
+            take_cross(*arrivals[k])
         if k == 1:
-            for n in xfac:
-                start_cross(n)
+            start_cross(7, 8, 9)
+        if k == 2:
+            start_cross(15, 16, 17)
 
         def assemble(lo, hi, piece):
             @pl.loop(lo, hi)
@@ -219,25 +233,29 @@
                 both = ca[rows, cols(j)].astype(F32) + cb[rows, cols(j)].astype(F32)
                 apan[:, cols(j)] = both + piece(j)
 
-        if k < 3:
-            @pl.when(par == 0)
-            def _():
-                assemble(k, STEPS, lambda j: og[rows, cols(j)].astype(F32))
-
-            @pl.when(par == 1)
-            def _():
-                assemble(k, 3, lambda j: ox[rows, cols(j)].astype(F32))
-                assemble(3, STEPS, lambda j: og[cols(j - 3), rows].astype(F32).T)
-        else:
-            part = slice(rows.start - HALF, rows.stop - HALF)
-
-            @pl.when(par == 0)
-            def _():
-                assemble(k, STEPS, lambda j: ox[part, cols(j - 3)].astype(F32))
-
-            @pl.when(par == 1)
-            def _():
-                assemble(k, STEPS, lambda j: og[part, cols(j)].astype(F32))
+        def assemble_all(lo, hi):
+            if k < 3:
+                @pl.when(par == 0)
+                def _():
+                    assemble(lo, hi, lambda j: og[rows, cols(j)].astype(F32))
+
+                @pl.when(par == 1)
+                def _():
+                    assemble(lo, min(hi, 3), lambda j: ox[rows, cols(j)].astype(F32))
+                    if hi > 3:
+                        assemble(3, hi, lambda j: og[cols(j - 3), rows].astype(F32).T)
+            else:
+                part = slice(rows.start - HALF, rows.stop - HALF)
+
+                @pl.when(par == 0)
+                def _():
+                    assemble(lo, hi, lambda j: ox[part, cols(j - 3)].astype(F32))
+
+                @pl.when(par == 1)
+                def _():
+                    assemble(lo, hi, lambda j: og[part, cols(j)].astype(F32))
+
+        assemble_all(k, STEPS if k > 0 else 1)
 
         def updated(j):
             block = apan[:, cols(j)]
@@ -251,12 +269,24 @@
         w_ref[...] = eye()
         apan[:, rows] = diag
         factor_128(r_ref, w_ref, u_a, x_a)
+        if k == 1:
+            start_cross(10)
+        if k == 5:
+            take_cross(13, 14, 15, 16, 17)
         xa = x_a[...]
         uab = dot_split(xa, apan[0:H, rows.start + H : rows.stop])
         lba = uab.T
         r_ref[...] = apan[H:NB, rows.start + H : rows.stop] - dot_split(lba, uab)
         w_ref[...] = eye()
         factor_128(r_ref, w_ref, u_b, x_b)
+        if k == 0:
+            start_cross(4, 5, 6)
+            wait_own(2, 3, 4, 5)
+            take_cross(2, 3)
+            assemble_all(1, STEPS)
+            start_own(11, 12, 13, 14, 15)
+        if k == 1:
+            start_cross(11, 12, 13, 14)
         xf[0:H, 0:H] = xa
         xf[0:H, H:NB] = jnp.zeros((H, H), F32)
         xf[H:NB, 0:H] = -dot_split(x_b[...], dot_split(lba, xa))
@@ -282,13 +312,21 @@
                 lh[cols(j), rows] = thi
                 ll[cols(j), rows] = tlo
 
+            below = rows.stop
+            for ref, dst in ((lh, lh_out), (ll, ll_out)):
+                copy = pltpu.make_async_copy(
+                    box(ref, below, N - below, rows.start, NB),
+                    box(dst, below, N - below, rows.start, NB),
+                    out_sem.at[len(writes)],
+                )
+                copy.start()
+                writes.append(copy)
+
     mine = pl.ds(pl.multiple_of(par * HALF + core * QUARTER, 128), QUARTER)
-    write = pltpu.make_async_copy(lf.at[mine, :], out_lead, out_sem)
+    write = pltpu.make_async_copy(lf.at[mine, :], out_lead, out_sem.at[len(writes)])
     write.start()
-    for n in xfac:
-        take_cross(n)
-    for n in fac:
-        wait_own(n)
+    writes.append(write)
+    wait_own(11, 12, 13, 14, 15)
     for n in range(len(own)):
         @pl.when(core == own[n][0])
         def _():
@@ -298,7 +336,8 @@
         def _():
             to_peer(n).wait_send()
             relay(n).wait_send()
-    write.wait()
+    for copy in writes:
+        copy.wait()
 
 
 def factor_call(child, orig, fl, fr, op):
@@ -318,7 +357,7 @@
             jax.ShapeDtypeStruct((N, 512), BF16),
         ),
         in_specs=[any_spec] * 5,
-        out_specs=(any_spec, vmem, vmem, vmem, vmem, any_spec, any_spec, any_spec),
+        out_specs=(any_spec, any_spec, any_spec, vmem, vmem, any_spec, any_spec, any_spec),
         scratch_shapes=[
             pltpu.VMEM((N, N), BF16),
             pltpu.VMEM((N, N), BF16),
@@ -328,10 +367,12 @@
             pltpu.VMEM((N, N), F32),
             pltpu.VMEM((N, N), BF16),
             pltpu.VMEM((N, N), BF16),
+            pltpu.VMEM((N, N), BF16),
+            pltpu.VMEM((N, N), BF16),
             pltpu.VMEM((NB, NB), F32),
         ]
         + [pltpu.VMEM((H, H), F32)] * 6
-        + [dma((13,)), dma((13,)), dma((13,)), dma((17,)), dma((17,)), dma((17,)), dma(())],
+        + [dma((16,)), dma((16,)), dma((16,)), dma((18,)), dma((18,)), dma((18,)), dma((11,))],
         compiler_params=pltpu.CompilerParams(
             collective_id=0, has_side_effects=True, vmem_limit_bytes=56 << 20
         ),
@@ -339,27 +380,60 @@
     )(child, orig, fl, fr, op)
 
 
-def solve_kernel(lh, ll, xh, xl, fl, fr, op, panel, mask, onext, upper, below, rh, rl, wt):
+def solve_kernel(
+    place, lh_in, ll_in, fl_in, op_in, xh, xl, fr, panel, mask, onext, upper, below,
+    lh, ll, fl, op, rh, wt, sems,
+):
     step = pl.program_id(0)
     width = panel.shape[1]
-    right = jnp.concatenate([fr[...] * mask[0, o : o + 1, :] for o in range(width // NB)], axis=0)
-
-    def orig_rows(rows):
-        return jnp.where(step == 0, op[rows, :], panel[rows, :]).astype(F32)
+
+    def loads(k):
+        rows = pl.ds(k * NB, NB)
+        pairs = [(fl_in.at[rows, :], fl.at[rows, :]), (op_in.at[rows, :], op.at[rows, :])]
+        if k > 0:
+            done = pl.ds(0, k * NB)
+            pairs += [(lh_in.at[rows, done], lh.at[rows, done]), (ll_in.at[rows, done], ll.at[rows, done])]
+        return [pltpu.make_async_copy(src, dst, sems.at[k, n]) for n, (src, dst) in enumerate(pairs)]
+
+    @pl.when(step == 0)
+    def _():
+        for k in range(STEPS):
+            for copy in loads(k):
+                copy.start()
+
+    spots, rights = [], []
+    for o in range(width // NB):
+        spot = [pl.ds(pl.multiple_of(place[step, 2 * o + c] * H, H), H) for c in range(2)]
+        spots.append(spot)
+        rights.append(jnp.concatenate([fr[:, s] * mask[0, o : o + 1, c * H : c * H + H] for c, s in enumerate(spot)], axis=1))
 
     for k in range(STEPS):
         rows = slice(k * NB, (k + 1) * NB)
-        acc = orig_rows(rows) + lax.dot_general(
-            fl[rows, :], right, (((1,), (1,)), ((), ())), preferred_element_type=F32
+
+        @pl.when(step == 0)
+        def _():
+            for copy in loads(k):
+                copy.wait()
+
+        spread = jnp.concatenate(
+            [
+                lax.dot_general(
+                    jnp.concatenate([fl[rows, s] for s in spot], axis=1),
+                    right,
+                    (((1,), (1,)), ((), ())),
+                    preferred_element_type=F32,
+                )
+                for spot, right in zip(spots, rights)
+            ],
+            axis=1,
         )
+        acc = jnp.where(step == 0, op[rows, :], panel[rows, :]).astype(F32) + spread
         if k > 0:
             done = slice(0, k * NB)
-            acc = acc - dot3(lh[rows, done], ll[rows, done], rh[done, :], rl[done, :])
+            acc = acc - (dot(lh[rows, done], rh[done, :]) + dot(ll[rows, done], rh[done, :]))
         bh, bl = split(acc)
         u = dot3(xh[rows, :], xl[rows, :], bh, bl)
-        uhi, ulo = split(u)
-        rh[rows, :] = uhi
-        rl[rows, :] = ulo
+        rh[rows, :] = u.astype(BF16)
         upper[rows, :] = u
 
         @pl.when(step == 0)
@@ -371,34 +445,43 @@
         below[...] = onext[...].astype(F32) - dot(wt[...], rh[...])
 
 
-def solve_call(lh, ll, xh, xl, fl, fr, op, panel, mask, onext):
+def solve_call(place, lh, ll, xh, xl, fl, fr, op, panel, mask, onext):
     width = 512
     count = panel.shape[1] // width
+    any_spec = pl.BlockSpec(memory_space=pl.ANY)
 
     def whole(x):
-        return pl.BlockSpec(x.shape, lambda t: (0, 0), pipeline_mode=pl.Buffered(1))
+        return pl.BlockSpec(x.shape, lambda t, p: (0, 0), pipeline_mode=pl.Buffered(1))
 
     def tile(x):
-        return pl.BlockSpec((x.shape[0], width), lambda t: (0, jnp.maximum(t - 1, 0)))
+        return pl.BlockSpec((x.shape[0], width), lambda t, p: (0, jnp.maximum(t - 1, 0)))
 
     return pl.pallas_call(
         solve_kernel,
-        grid=(count + 1,),
         out_shape=(
             jax.ShapeDtypeStruct(panel.shape, F32),
             jax.ShapeDtypeStruct(onext.shape, F32),
         ),
-        in_specs=[whole(x) for x in (lh, ll, xh, xl, fl, fr, op)]
-        + [tile(panel), pl.BlockSpec((1, 2, 1024), lambda t: (t, 0, 0)), tile(onext)],
-        out_specs=(tile(panel), tile(onext)),
-        scratch_shapes=[
-            pltpu.VMEM((N, width), BF16),
-            pltpu.VMEM((N, width), BF16),
-            pltpu.VMEM((512, N), BF16),
-        ],
+        grid_spec=pltpu.PrefetchScalarGridSpec(
+            num_scalar_prefetch=1,
+            grid=(count + 1,),
+            in_specs=[any_spec] * 4
+            + [whole(x) for x in (xh, xl, fr)]
+            + [tile(panel), pl.BlockSpec((1, 2, 2 * H), lambda t, p: (t, 0, 0)), tile(onext)],
+            out_specs=(tile(panel), tile(onext)),
+            scratch_shapes=[
+                pltpu.VMEM((N, N), BF16),
+                pltpu.VMEM((N, N), BF16),
+                pltpu.VMEM((N, 1024), BF16),
+                pltpu.VMEM((N, 512), BF16),
+                pltpu.VMEM((N, width), BF16),
+                pltpu.VMEM((512, N), BF16),
+                pltpu.SemaphoreType.DMA((STEPS, 4)),
+            ],
+        ),
         compiler_params=pltpu.CompilerParams(vmem_limit_bytes=56 << 20),
         name="solve",
-    )(lh, ll, xh, xl, fl, fr, op, panel, mask, onext)
+    )(place, lh, ll, fl, op, xh, xl, fr, panel, mask, onext)
 
 
 def shards(fac_left, fac_right, block_rank, col_map, child_lead, orig_lead, orig_panel, orig_next):
@@ -411,10 +494,13 @@
     targets = jnp.concatenate([jnp.array([0, 8], jnp.int32), own])
     maps = lax.dynamic_slice_in_dim(col_map, leaf - par, 2, 0).reshape(16)
     ranks = lax.dynamic_slice_in_dim(block_rank, leaf - par, 2, 0).reshape(16)
-    live = jnp.arange(RMAX)[None, :] < ranks[:, None]
-    hit = targets[:, None] == maps[None, :]
-    mask = (hit[:, :, None] & live[None]).astype(BF16).reshape(3, 2, 1024)
-    upper, below = solve_call(lh, ll, xh, xl, flg, frg, opg, orig_panel[0], mask, orig_next[0])
+    hit = (targets[:, None] == maps[None, :]).reshape(6, 2, 8)
+    pair = jnp.sum(jnp.where(hit, jnp.arange(8, dtype=jnp.int32) // 2, 0), axis=2)
+    place = (pair + jnp.array([[0, 4]], jnp.int32)).reshape(3, 4)
+    live = (jnp.arange(RMAX)[None, :] < ranks[:, None]).reshape(1, 2, 8, RMAX)
+    used = (hit[..., None] & live).reshape(6, 2, 4, 2 * RMAX)
+    mask = jnp.any(used, axis=2).astype(BF16).reshape(3, 2, 4 * RMAX)
+    upper, below = solve_call(place, lh, ll, xh, xl, flg, frg, opg, orig_panel[0], mask, orig_next[0])
     return (out_lead[None], upper[None], below[None])
 
 

time: 141 us -> 132 us (0.936)
  Pallas kernels: 135 us -> 126 us
    pallas_call x1, Pallas kernels: 35.6 us -> 26.9 us  [solve_call(): pl.pallas_call(solve_kernel, out_shape=(jax.ShapeDtypeStruct(panel.shape,...]
where the time goes in v3:
time: 132 us; the launch traced here: 131 us
  Pallas kernels  126 us (95%)
  local copies, waits for them, and re-layouts  3.51 us (3%)
    pallas_call x1, Pallas kernels, factor_call(): pl.pallas_call(factor_kernel, out_shape=(jax.ShapeDtypeStruct((QUARTER, N...  99.2 us
    pallas_call x1, Pallas kernels, solve_call(): pl.pallas_call(solve_kernel, out_shape=(jax.ShapeDtypeStruct(panel.shape,...  26.9 us

profile of v3, /device:TPU:1, one launch (start us, length us, event | category | flops | bytes accessed | tf_op | source)
XLA Modules:
  0.0 131.4 jit_solution(12109155689708425725)
XLA Ops:
  0.7 0.1 pad_add_fusion
  0.8 0.1 add.40
  0.8 0.1 lt.36
  0.9 0.8 constant_dynamic-slice_fusion
  1.7 0.1 copy.18
  1.8 0.1 copy.17
  1.9 0.1 broadcast_compare_fusion
  1.9 0.2 select_reduce_fusion
  2.2 0.1 reduce_sum.12
  2.3 0.6 broadcast_add_fusion.place
  2.9 0.1 lt.38
  2.9 0.1 lt.39
  3.0 0.1 and.30
  3.1 0.1 and.31
  3.3 0.6 reshape.55.mask
  3.9 99.2 %factor.1 = (f32[384,1536]{1,0:T(8,128)}, bf16[1536,1536]{1,0:T(8,128)(2,1)}, bf16[1536,1536]{1,0:T(8,128)(2,1)}, bf16[1536,256]{1,0:T(8,128)(2,1)}, bf16[1536,2...) custom-call(bf16[768,1536]{1,0:T(8,128)(2,1)} %bitcast.14, ...), custom_call_target="tpu_custom_call" | custom-call | tf_op jit(solution)/shard_map/factor/pallas_call | solution.py:347
  103.0 0.0 copy-start
  103.0 26.9 %solve.1 = (f32[1536,1024]{1,0:T(8,128)}, f32[512,1024]{1,0:T(8,128)}) custom-call(s32[3,4]{1,0:T(4,128)} %broadcast_add_fusion.place, bf16[1536,1536]{1,0:T(8,128)(2,1)} %get-tuple-element.14.lh_in, bf16[1536,1536]{1,0:T(8,128)(2,1)} %get-tuple-element.15.ll_in, bf16[1536,1024]{1,0:T(8,128)(2,1)} %get-tuple-element.16.fl_in, ...), custom_call_target="tpu_custom_call" | custom-call | tf_op jit(solution)/shard_map/solve/pallas_call | solution.py:459
  130.0 0.0 copy-done
  130.0 1.4 %copy.20 = f32[1,384,1536]{2,1,0:T(8,128)} copy(f32[1,384,1536]{2,1,0:T(8,128)S(1)} %bitcast.13) | data formatting | bytes 4718592
  (9 shorter events, 0.1 us)
Async XLA Ops:
  103.0 27.0 %copy-start = (f32[384,1536]{1,0:T(8,128)S(1)}, f32[384,1536]{1,0:T(8,128)}, u32[]{:S(2)}) copy-start(f32[384,1536]{1,0:T(8,128)} %get-tuple-element.13) | copy-start | bytes 7077892

commit v4 on v3

--- a/solution.py
+++ b/solution.py
@@ -89,14 +89,10 @@
     return jnp.where(col == low, 1.0, 0.0).astype(F32)
 
 
-def cols(j):
-    return pl.ds(pl.multiple_of(j * NB, NB), NB)
-
-
 def factor_kernel(
     child, orig, fl, fr, op,
     out_lead, lh_out, ll_out, xh, xl, flg, frg, opg,
-    ca, cb, og, ox, apan, lf, lh, ll, uh, ul, xf, r_ref, w_ref, u_a, x_a, u_b, x_b,
+    ca, cb, og, ox, acol, lf, lh, ll, uh, ul, xf, r_ref, w_ref, u_a, x_a, u_b, x_b,
     loc, sib_send, sib_recv, x_send, relay_send, x_recv, out_sem,
 ):
     leaf, core = lax.axis_index("leaf"), lax.axis_index("front")
@@ -115,50 +111,52 @@
         return ref.at[pl.ds(row, height), pl.ds(col, width)]
 
     own = [
-        (0, box(child, 0, NB, 0, NB), box(ca, 0, NB, 0, NB)),
         (0, box(orig, 0, NB, 0, NB), box(og, 0, NB, 0, NB)),
-        (0, box(child, 0, NB, NB, N - NB), box(ca, 0, NB, NB, N - NB)),
         (0, box(orig, 0, NB, NB, N - NB), box(og, 0, NB, NB, N - NB)),
         (0, box(orig, NB, H, 0, N), box(og, NB, H, 0, N)),
         (1, orig, box(og, QUARTER, QUARTER, 0, N)),
     ]
-    for k in range(1, STEPS):
-        own.append((k // 3, box(child, k % 3 * NB, NB, k * NB, N - k * NB), box(ca, k * NB, NB, k * NB, N - k * NB)))
+    own_col, cross_col, cross = [], [], []
+    for k in range(STEPS):
+        own_col.append([len(own)])
+        high = min(NB * (k + 1), HALF)
+        own.append((0, box(child, 0, high, k * NB, NB), box(ca, 0, high, k * NB, NB)))
+        if k >= 3:
+            own_col[k].append(len(own))
+            own.append((1, box(child, 0, NB * (k - 2), k * NB, NB), box(ca, HALF, NB * (k - 2), k * NB, NB)))
+    own_fac = tuple(range(len(own), len(own) + 5))
     for c in range(2):
         own.append((c, fl, slot(flg, 2 * par + c, 256)))
     for c in range(2):
         own.append((c, fr, slot(frg, 2 * par + c, 256)))
     own.append((0, op.at[:, pl.ds(0, NB)], slot(opg, par, NB)))
 
-    def square(c, row, height, start, width):
-        src = box(orig, row, height, pl.multiple_of(par * HALF + start, 128), width)
-        there = box(ox, c * QUARTER + row, height, start, width)
-        return (c, src, there, there)
-
-    def lead_item(k, start, width):
-        src = box(child, k % 3 * NB, NB, start, width)
-        there = box(cb, k * NB, NB, start, width)
-        return (k // 3, src, there, there)
-
-    cross = [
-        lead_item(0, 0, NB),
-        square(0, 0, NB, 0, NB),
-        lead_item(0, NB, N - NB),
-        square(0, 0, NB, NB, HALF - NB),
-        lead_item(1, NB, N - NB),
-        square(0, NB, H, NB, HALF - NB),
-        square(1, 0, H, QUARTER, QUARTER),
-        lead_item(2, 2 * NB, N - 2 * NB),
-        square(1, H, H, QUARTER + H, QUARTER - H),
-        square(1, 2 * H, H, QUARTER + 2 * H, H),
-    ]
-    for k in range(3, STEPS):
-        cross.append(lead_item(k, k * NB, N - k * NB))
+    def square(c, height, k):
+        src = box(orig, 0, height, pl.multiple_of(par * HALF + k * NB, 128), NB)
+        there = box(ox, c * QUARTER, height, k * NB, NB)
+        cross_col[k].append(len(cross))
+        cross.append((c, src, there, there))
+
+    for k in range(STEPS):
+        high = min(NB * (k + 1), HALF)
+        cross_col.append([len(cross)])
+        there = box(cb, 0, high, k * NB, NB)
+        cross.append((0, box(child, 0, high, k * NB, NB), there, there))
+        if k >= 3:
+            there = box(cb, HALF, NB * (k - 2), k * NB, NB)
+            cross_col[k].append(len(cross))
+            cross.append((1, box(child, 0, NB * (k - 2), k * NB, NB), there, there))
+        else:
+            square(0, min(NB * (k + 1), QUARTER), k)
+            if k > 0:
+                square(1, NB * (k + 1) - QUARTER, k)
+    first = len(cross)
     for c in range(2):
         cross.append((c, fl, slot(flg, 2 * par + c, 256), slot(flg, 2 * (1 - par) + c, 256)))
     for c in range(2):
         cross.append((c, fr, slot(frg, 2 * par + c, 256), slot(frg, 2 * (1 - par) + c, 256)))
     cross.append((0, op.at[:, pl.ds(0, NB)], slot(opg, par, NB), slot(opg, 1 - par, NB)))
+    cross_fl, cross_rest = (first, first + 1), (first + 2, first + 3, first + 4)
 
     def local(n):
         return pltpu.make_async_copy(own[n][1], own[n][2], loc.at[n])
@@ -198,135 +196,135 @@
             def _():
                 to_peer(n).start()
 
-    def take_cross(*items):
+    def pass_on(*items):
         for n in items:
-            relay(n).wait_recv()
-
             @pl.when(core == cross[n][0])
             def _():
+                relay(n).wait_recv()
                 relay(n).start()
 
-    start_cross(0, 1)
-    start_own(0, 1, 2, 3, 4, 5)
+    def take(*items):
+        for n in items:
+            @pl.when(core != cross[n][0])
+            def _():
+                relay(n).wait_recv()
+
+    start_cross(*cross_col[0])
+    start_own(0, *own_col[0])
     for k in range(STEPS):
         lf[pl.ds(k * NB, NB), :] = jnp.zeros((NB, N), F32)
-    wait_own(0, 1)
-    take_cross(0, 1)
-    start_cross(2, 3)
-    start_own(6, 7, 8, 9, 10)
-
-    arrivals = {1: (4, 5, 6), 2: (7, 8, 9), 3: (10,), 4: (11,), 5: (12,)}
+    pass_on(*cross_col[0])
+    start_cross(*cross_col[1])
+    start_own(1, 2, 3)
+    for k in range(1, STEPS):
+        start_own(*own_col[k])
+
     writes = []
     for k in range(STEPS):
         rows = slice(k * NB, (k + 1) * NB)
+        wait_own(*own_col[k])
+        wait_own(*{0: (0,), 1: (1, 2, 3)}.get(k, ()))
+        take(*cross_col[k])
+        if k == 1:
+            start_cross(*cross_col[4])
+        if k == 2:
+            start_cross(*cross_fl)
+            start_own(*own_fac)
+        if k == 3:
+            start_cross(*cross_rest)
+
+        def assemble(lo, hi, piece):
+            for i in range(lo, hi):
+                part = slice(i * NB, (i + 1) * NB)
+                both = ca[part, rows].astype(F32) + cb[part, rows].astype(F32)
+                acol[part, :] = both + piece(i)
+
+        def lower(ref, i, j):
+            return ref[i * NB : (i + 1) * NB, j * NB : (j + 1) * NB].astype(F32)
+
+        @pl.when(par == 0)
+        def _():
+            assemble(0, min(k + 1, 3), lambda i: lower(og, i, k))
+            assemble(3, k + 1, lambda i: lower(ox, i - 3, k - 3))
+
+        @pl.when(par == 1)
+        def _():
+            if k < 3:
+                assemble(0, k + 1, lambda i: lower(ox, i, k))
+            else:
+                assemble(0, 3, lambda i: lower(og, k - 3, i).T)
+                assemble(3, k + 1, lambda i: lower(og, i - 3, k))
+
+        def updated(i):
+            part = slice(i * NB, (i + 1) * NB)
+            if i == 0:
+                return acol[part, :]
+            done = slice(0, i * NB)
+            return acol[part, :] - dot3(lh[part, done], ll[part, done], uh[done, :], ul[done, :])
+
+        for i in range(k):
+            part = slice(i * NB, (i + 1) * NB)
+            bh, bl = split(updated(i))
+            u = dot3(xh[part, :], xl[part, :], bh, bl)
+            uhi, ulo = split(u)
+            uh[part, :] = uhi
+            ul[part, :] = ulo
+            t = u.T
+            lf[rows, part] = t
+            thi, tlo = split(t)
+            lh[rows, part] = thi
+            ll[rows, part] = tlo
         if k > 0:
-            wait_own(5 + k)
-            take_cross(*arrivals[k])
-        if k == 1:
-            start_cross(7, 8, 9)
-        if k == 2:
-            start_cross(15, 16, 17)
-
-        def assemble(lo, hi, piece):
-            @pl.loop(lo, hi)
-            def _(j):
-                both = ca[rows, cols(j)].astype(F32) + cb[rows, cols(j)].astype(F32)
-                apan[:, cols(j)] = both + piece(j)
-
-        def assemble_all(lo, hi):
-            if k < 3:
-                @pl.when(par == 0)
-                def _():
-                    assemble(lo, hi, lambda j: og[rows, cols(j)].astype(F32))
-
-                @pl.when(par == 1)
-                def _():
-                    assemble(lo, min(hi, 3), lambda j: ox[rows, cols(j)].astype(F32))
-                    if hi > 3:
-                        assemble(3, hi, lambda j: og[cols(j - 3), rows].astype(F32).T)
-            else:
-                part = slice(rows.start - HALF, rows.stop - HALF)
-
-                @pl.when(par == 0)
-                def _():
-                    assemble(lo, hi, lambda j: ox[part, cols(j - 3)].astype(F32))
-
-                @pl.when(par == 1)
-                def _():
-                    assemble(lo, hi, lambda j: og[part, cols(j)].astype(F32))
-
-        assemble_all(k, STEPS if k > 0 else 1)
-
-        def updated(j):
-            block = apan[:, cols(j)]
-            if k == 0:
-                return block
-            done = slice(0, k * NB)
-            return block - dot3(lh[rows, done], ll[rows, done], uh[done, cols(j)], ul[done, cols(j)])
+            for ref, dst in ((lh, lh_out), (ll, ll_out)):
+                copy = pltpu.make_async_copy(
+                    box(ref, rows.start, NB, 0, k * NB),
+                    box(dst, rows.start, NB, 0, k * NB),
+                    out_sem.at[len(writes)],
+                )
+                copy.start()
+                writes.append(copy)
 
         diag = updated(k)
+        acol[rows, :] = diag
         r_ref[...] = diag[:H, :H]
         w_ref[...] = eye()
-        apan[:, rows] = diag
         factor_128(r_ref, w_ref, u_a, x_a)
+        if k == 0:
+            start_cross(*cross_col[2])
         if k == 1:
-            start_cross(10)
-        if k == 5:
-            take_cross(13, 14, 15, 16, 17)
+            start_cross(*cross_col[5])
+        if k < STEPS - 1:
+            pass_on(*cross_col[k + 1])
+        if k == STEPS - 1:
+            pass_on(*cross_fl)
+        mid = rows.start + H
         xa = x_a[...]
-        uab = dot_split(xa, apan[0:H, rows.start + H : rows.stop])
+        uab = dot_split(xa, acol[rows.start : mid, H:NB])
         lba = uab.T
-        r_ref[...] = apan[H:NB, rows.start + H : rows.stop] - dot_split(lba, uab)
+        r_ref[...] = acol[mid : rows.stop, H:NB] - dot_split(lba, uab)
         w_ref[...] = eye()
         factor_128(r_ref, w_ref, u_b, x_b)
         if k == 0:
-            start_cross(4, 5, 6)
-            wait_own(2, 3, 4, 5)
-            take_cross(2, 3)
-            assemble_all(1, STEPS)
-            start_own(11, 12, 13, 14, 15)
-        if k == 1:
-            start_cross(11, 12, 13, 14)
+            start_cross(*cross_col[3])
+        if k == STEPS - 1:
+            pass_on(*cross_rest)
         xf[0:H, 0:H] = xa
         xf[0:H, H:NB] = jnp.zeros((H, H), F32)
         xf[H:NB, 0:H] = -dot_split(x_b[...], dot_split(lba, xa))
         xf[H:NB, H:NB] = x_b[...]
-        mid = rows.start + H
         lf[rows.start : mid, rows.start : mid] = u_a[...].T
         lf[mid : rows.stop, rows.start : mid] = lba
         lf[mid : rows.stop, mid : rows.stop] = u_b[...].T
         hi, lo = split(xf[...])
         xh[rows, :] = hi
         xl[rows, :] = lo
-        if k < STEPS - 1:
-            @pl.loop(k + 1, STEPS)
-            def _(j):
-                bh, bl = split(updated(j))
-                u = dot3(xh[rows, :], xl[rows, :], bh, bl)
-                uhi, ulo = split(u)
-                uh[rows, cols(j)] = uhi
-                ul[rows, cols(j)] = ulo
-                t = u.T
-                lf[cols(j), rows] = t
-                thi, tlo = split(t)
-                lh[cols(j), rows] = thi
-                ll[cols(j), rows] = tlo
-
-            below = rows.stop
-            for ref, dst in ((lh, lh_out), (ll, ll_out)):
-                copy = pltpu.make_async_copy(
-                    box(ref, below, N - below, rows.start, NB),
-                    box(dst, below, N - below, rows.start, NB),
-                    out_sem.at[len(writes)],
-                )
-                copy.start()
-                writes.append(copy)
 
     mine = pl.ds(pl.multiple_of(par * HALF + core * QUARTER, 128), QUARTER)
     write = pltpu.make_async_copy(lf.at[mine, :], out_lead, out_sem.at[len(writes)])
     write.start()
     writes.append(write)
-    wait_own(11, 12, 13, 14, 15)
+    wait_own(*own_fac)
+    take(*cross_fl, *cross_rest)
     for n in range(len(own)):
         @pl.when(core == own[n][0])
         def _():
@@ -363,16 +361,16 @@
             pltpu.VMEM((N, N), BF16),
             pltpu.VMEM((HALF, N), BF16),
             pltpu.VMEM((HALF, HALF), BF16),
-            pltpu.VMEM((NB, N), F32),
+            pltpu.VMEM((N, NB), F32),
             pltpu.VMEM((N, N), F32),
             pltpu.VMEM((N, N), BF16),
             pltpu.VMEM((N, N), BF16),
-            pltpu.VMEM((N, N), BF16),
-            pltpu.VMEM((N, N), BF16),
+            pltpu.VMEM((N, NB), BF16),
+            pltpu.VMEM((N, NB), BF16),
             pltpu.VMEM((NB, NB), F32),
         ]
         + [pltpu.VMEM((H, H), F32)] * 6
-        + [dma((16,)), dma((16,)), dma((16,)), dma((18,)), dma((18,)), dma((18,)), dma((11,))],
+        + [dma((18,)), dma((18,)), dma((18,)), dma((19,)), dma((19,)), dma((19,)), dma((11,))],
         compiler_params=pltpu.CompilerParams(
             collective_id=0, has_side_effects=True, vmem_limit_bytes=56 << 20
         ),

time: 132 us -> 120 us (0.909)
  the two profiles are of different devices: /device:TPU:1 before, /device:TPU:0 now
where the time goes in v4:
time: 120 us
  Pallas kernels  114 us (95%)
  local copies, waits for them, and re-layouts  3.51 us (3%)
    pallas_call x1, Pallas kernels, factor_call(): pl.pallas_call(factor_kernel, out_shape=(jax.ShapeDtypeStruct((QUARTER, N...  87.4 us
    pallas_call x1, Pallas kernels, solve_call(): pl.pallas_call(solve_kernel, out_shape=(jax.ShapeDtypeStruct(panel.shape,...  26.9 us

profile of v4, /device:TPU:0, one launch (start us, length us, event | category | flops | bytes accessed | tf_op | source)
XLA Modules:
  0.0 119.6 jit_solution(3596352966745064743)
XLA Ops:
  0.7 0.1 pad_add_fusion
  0.8 0.1 add.40
  0.8 0.1 lt.36
  0.9 0.8 constant_dynamic-slice_fusion
  1.7 0.1 copy.18
  1.8 0.1 copy.17
  1.9 0.1 broadcast_compare_fusion
  1.9 0.2 select_reduce_fusion
  2.2 0.1 reduce_sum.12
  2.3 0.6 broadcast_add_fusion.place
  2.9 0.1 lt.38
  2.9 0.1 lt.39
  3.0 0.1 and.30
  3.1 0.1 and.31
  3.3 0.6 reshape.55.mask
  3.9 87.4 %factor.1 = (f32[384,1536]{1,0:T(8,128)}, bf16[1536,1536]{1,0:T(8,128)(2,1)}, bf16[1536,1536]{1,0:T(8,128)(2,1)}, bf16[1536,256]{1,0:T(8,128)(2,1)}, bf16[1536,2...) custom-call(bf16[768,1536]{1,0:T(8,128)(2,1)} %bitcast.14, ...), custom_call_target="tpu_custom_call" | custom-call | tf_op jit(solution)/shard_map/factor/pallas_call | solution.py:345
  91.2 0.0 copy-start
  91.3 26.9 %solve.1 = (f32[1536,1024]{1,0:T(8,128)}, f32[512,1024]{1,0:T(8,128)}) custom-call(s32[3,4]{1,0:T(4,128)} %broadcast_add_fusion.place, bf16[1536,1536]{1,0:T(8,128)(2,1)} %get-tuple-element.14.lh_in, bf16[1536,1536]{1,0:T(8,128)(2,1)} %get-tuple-element.15.ll_in, bf16[1536,1024]{1,0:T(8,128)(2,1)} %get-tuple-element.16.fl_in, ...), custom_call_target="tpu_custom_call" | custom-call | tf_op jit(solution)/shard_map/solve/pallas_call | solution.py:457
  118.2 0.0 copy-done
  118.2 1.4 %copy.20 = f32[1,384,1536]{2,1,0:T(8,128)} copy(f32[1,384,1536]{2,1,0:T(8,128)S(1)} %bitcast.13) | data formatting | bytes 4718592
  (9 shorter events, 0.1 us)
Async XLA Ops:
  91.2 27.0 %copy-start = (f32[384,1536]{1,0:T(8,128)S(1)}, f32[384,1536]{1,0:T(8,128)}, u32[]{:S(2)}) copy-start(f32[384,1536]{1,0:T(8,128)} %get-tuple-element.13) | copy-start | bytes 7077892

commit v5 on v4

--- a/solution.py
+++ b/solution.py
@@ -37,7 +37,7 @@
     return dot3(*split(a), *split(b))
 
 
-def factor_128(r_ref, x_ref, u_out, x_out):
+def factor_128(r_ref, x_ref, u_out, x_out, held):
     sub = lax.broadcasted_iota(jnp.int32, (W, H), 0)
 
     def panel(p, carry):
@@ -47,6 +47,7 @@
         inverses = jnp.ones((W, H), F32)
         for i in range(W):
             base = i // 8 * 8
+            held[i * W + base : (i + 1) * W, :] = col[i]
             pivot = col[i][i - base : i - base + 1, :]
             inv = 1.0 / pivot
             m = jnp.where(sub[base:] > i, col[i] * inv, 0.0)
@@ -54,7 +55,8 @@
             inverses = jnp.where(sub == i, inv, inverses)
             for k in range(i + 1, W):
                 low = k // 8 * 8
-                col[k] = col[k] - m[low - base :] * col[i][k - base : k - base + 1, :]
+                near = col[i][k - base : k - base + 1, :] if k == i + 1 else held[i * W + k : i * W + k + 1, :]
+                col[k] = col[k] - m[low - base :] * near
             row, xrow = top[i : i + 1, :], xtop[i : i + 1, :]
             ntop, nxtop = top[base:] - m * row, xtop[base:] - m * xrow
             top = ntop if base == 0 else jnp.concatenate([top[:base], ntop], axis=0)
@@ -92,7 +94,7 @@
 def factor_kernel(
     child, orig, fl, fr, op,
     out_lead, lh_out, ll_out, xh, xl, flg, frg, opg,
-    ca, cb, og, ox, acol, lf, lh, ll, uh, ul, xf, r_ref, w_ref, u_a, x_a, u_b, x_b,
+    ca, cb, og, ox, acol, lf, lh, ll, uh, ul, xf, r_ref, w_ref, u_a, x_a, u_b, x_b, held,
     loc, sib_send, sib_recv, x_send, relay_send, x_recv, out_sem,
 ):
     leaf, core = lax.axis_index("leaf"), lax.axis_index("front")
@@ -219,12 +221,67 @@
     for k in range(1, STEPS):
         start_own(*own_col[k])
 
+    def assemble(k):
+        buf = k % 2
+        right = slice(k * NB, (k + 1) * NB)
+
+        def fill(lo, hi, piece):
+            for i in range(lo, hi):
+                part = slice(i * NB, (i + 1) * NB)
+                both = ca[part, right].astype(F32) + cb[part, right].astype(F32)
+                acol[buf, part, :] = both + piece(i)
+
+        def lower(ref, i, j):
+            return ref[i * NB : (i + 1) * NB, j * NB : (j + 1) * NB].astype(F32)
+
+        @pl.when(par == 0)
+        def _():
+            fill(0, min(k + 1, 3), lambda i: lower(og, i, k))
+            fill(3, k + 1, lambda i: lower(ox, i - 3, k - 3))
+
+        @pl.when(par == 1)
+        def _():
+            if k < 3:
+                fill(0, k + 1, lambda i: lower(ox, i, k))
+            else:
+                fill(0, 3, lambda i: lower(og, k - 3, i).T)
+                fill(3, k + 1, lambda i: lower(og, i - 3, k))
+
+    def updated(k, i):
+        part = slice(i * NB, (i + 1) * NB)
+        if i == 0:
+            return acol[k % 2, part, :]
+        done = slice(0, i * NB)
+        return acol[k % 2, part, :] - dot3(lh[part, done], ll[part, done], uh[k % 2, done, :], ul[k % 2, done, :])
+
+    def eliminate(k, i):
+        rows = slice(k * NB, (k + 1) * NB)
+        part = slice(i * NB, (i + 1) * NB)
+        bh, bl = split(updated(k, i))
+        u = dot3(xh[part, :], xl[part, :], bh, bl)
+        uhi, ulo = split(u)
+        uh[k % 2, part, :] = uhi
+        ul[k % 2, part, :] = ulo
+        t = u.T
+        lf[rows, part] = t
+        thi, tlo = split(t)
+        lh[rows, part] = thi
+        ll[rows, part] = tlo
+
+    def ready(k):
+        wait_own(*own_col[k])
+        wait_own(*{0: (0,), 1: (1, 2, 3)}.get(k, ()))
+        take(*cross_col[k])
+        assemble(k)
+
+    AHEAD = 2
     writes = []
     for k in range(STEPS):
         rows = slice(k * NB, (k + 1) * NB)
-        wait_own(*own_col[k])
-        wait_own(*{0: (0,), 1: (1, 2, 3)}.get(k, ()))
-        take(*cross_col[k])
+        if k <= AHEAD:
+            ready(k)
+        if k == 0:
+            start_cross(*cross_col[2])
         if k == 1:
             start_cross(*cross_col[4])
         if k == 2:
@@ -232,48 +289,15 @@
             start_own(*own_fac)
         if k == 3:
             start_cross(*cross_rest)
-
-        def assemble(lo, hi, piece):
-            for i in range(lo, hi):
-                part = slice(i * NB, (i + 1) * NB)
-                both = ca[part, rows].astype(F32) + cb[part, rows].astype(F32)
-                acol[part, :] = both + piece(i)
-
-        def lower(ref, i, j):
-            return ref[i * NB : (i + 1) * NB, j * NB : (j + 1) * NB].astype(F32)
-
-        @pl.when(par == 0)
-        def _():
-            assemble(0, min(k + 1, 3), lambda i: lower(og, i, k))
-            assemble(3, k + 1, lambda i: lower(ox, i - 3, k - 3))
-
-        @pl.when(par == 1)
-        def _():
-            if k < 3:
-                assemble(0, k + 1, lambda i: lower(ox, i, k))
-            else:
-                assemble(0, 3, lambda i: lower(og, k - 3, i).T)
-                assemble(3, k + 1, lambda i: lower(og, i - 3, k))
-
-        def updated(i):
-            part = slice(i * NB, (i + 1) * NB)
-            if i == 0:
-                return acol[part, :]
-            done = slice(0, i * NB)
-            return acol[part, :] - dot3(lh[part, done], ll[part, done], uh[done, :], ul[done, :])
-
-        for i in range(k):
-            part = slice(i * NB, (i + 1) * NB)
-            bh, bl = split(updated(i))
-            u = dot3(xh[part, :], xl[part, :], bh, bl)
-            uhi, ulo = split(u)
-            uh[part, :] = uhi
-            ul[part, :] = ulo
-            t = u.T
-            lf[rows, part] = t
-            thi, tlo = split(t)
-            lh[rows, part] = thi
-            ll[rows, part] = tlo
+        if AHEAD <= k < STEPS - 1:
+            pass_on(*cross_col[k + 1])
+
+        for i in range(k - 1 if k > AHEAD else 0, k):
+            eliminate(k, i)
+        diag = updated(k, k)
+        acol[k % 2, rows, :] = diag
+        r_ref[...] = diag[:H, :H]
+        w_ref[...] = eye()
         if k > 0:
             for ref, dst in ((lh, lh_out), (ll, ll_out)):
                 copy = pltpu.make_async_copy(
@@ -283,34 +307,33 @@
                 )
                 copy.start()
                 writes.append(copy)
-
-        diag = updated(k)
-        acol[rows, :] = diag
-        r_ref[...] = diag[:H, :H]
-        w_ref[...] = eye()
-        factor_128(r_ref, w_ref, u_a, x_a)
+        factor_128(r_ref, w_ref, u_a, x_a, held)
         if k == 0:
-            start_cross(*cross_col[2])
+            start_cross(*cross_col[3])
         if k == 1:
             start_cross(*cross_col[5])
-        if k < STEPS - 1:
+        if k < AHEAD:
             pass_on(*cross_col[k + 1])
         if k == STEPS - 1:
             pass_on(*cross_fl)
+        if AHEAD <= k < STEPS - 1:
+            ready(k + 1)
         mid = rows.start + H
         xa = x_a[...]
-        uab = dot_split(xa, acol[rows.start : mid, H:NB])
+        uab = dot_split(xa, acol[k % 2, rows.start : mid, H:NB])
         lba = uab.T
-        r_ref[...] = acol[mid : rows.stop, H:NB] - dot_split(lba, uab)
+        r_ref[...] = acol[k % 2, mid : rows.stop, H:NB] - dot_split(lba, uab)
         w_ref[...] = eye()
-        factor_128(r_ref, w_ref, u_b, x_b)
-        if k == 0:
-            start_cross(*cross_col[3])
+        below_a = dot_split(lba, xa)
+        if AHEAD <= k < STEPS - 1:
+            for i in range(k):
+                eliminate(k + 1, i)
+        factor_128(r_ref, w_ref, u_b, x_b, held)
         if k == STEPS - 1:
             pass_on(*cross_rest)
         xf[0:H, 0:H] = xa
         xf[0:H, H:NB] = jnp.zeros((H, H), F32)
-        xf[H:NB, 0:H] = -dot_split(x_b[...], dot_split(lba, xa))
+        xf[H:NB, 0:H] = -dot_split(x_b[...], below_a)
         xf[H:NB, H:NB] = x_b[...]
         lf[rows.start : mid, rows.start : mid] = u_a[...].T
         lf[mid : rows.stop, rows.start : mid] = lba
@@ -361,15 +384,16 @@
             pltpu.VMEM((N, N), BF16),
             pltpu.VMEM((HALF, N), BF16),
             pltpu.VMEM((HALF, HALF), BF16),
-            pltpu.VMEM((N, NB), F32),
+            pltpu.VMEM((2, N, NB), F32),
             pltpu.VMEM((N, N), F32),
             pltpu.VMEM((N, N), BF16),
             pltpu.VMEM((N, N), BF16),
-            pltpu.VMEM((N, NB), BF16),
-            pltpu.VMEM((N, NB), BF16),
+            pltpu.VMEM((2, N, NB), BF16),
+            pltpu.VMEM((2, N, NB), BF16),
             pltpu.VMEM((NB, NB), F32),
         ]
         + [pltpu.VMEM((H, H), F32)] * 6
+        + [pltpu.VMEM((W * W, H), F32)]
         + [dma((18,)), dma((18,)), dma((18,)), dma((19,)), dma((19,)), dma((19,)), dma((11,))],
         compiler_params=pltpu.CompilerParams(
             collective_id=0, has_side_effects=True, vmem_limit_bytes=56 << 20
@@ -379,107 +403,111 @@
 
 
 def solve_kernel(
-    place, lh_in, ll_in, fl_in, op_in, xh, xl, fr, panel, mask, onext, upper, below,
-    lh, ll, fl, op, rh, wt, sems,
+    place, lh_in, ll_in, fl_in, op_in, panel_in, onext_in, xh, xl, fr, mask, upper_out, below_out,
+    lh, ll, fl, op, panel, onext, rh, wt, upper, below, sems, next_sem, out_sem,
 ):
-    step = pl.program_id(0)
-    width = panel.shape[1]
+    lead, width = op.shape[1], panel.shape[1]
+    tile = 512
+    total = lead + width
 
     def loads(k):
         rows = pl.ds(k * NB, NB)
-        pairs = [(fl_in.at[rows, :], fl.at[rows, :]), (op_in.at[rows, :], op.at[rows, :])]
+        pairs = [(fl_in.at[rows, :], fl.at[rows, :]), (op_in.at[rows, :], op.at[rows, :]),
+                 (panel_in.at[rows, :], panel.at[rows, :])]
         if k > 0:
             done = pl.ds(0, k * NB)
             pairs += [(lh_in.at[rows, done], lh.at[rows, done]), (ll_in.at[rows, done], ll.at[rows, done])]
         return [pltpu.make_async_copy(src, dst, sems.at[k, n]) for n, (src, dst) in enumerate(pairs)]
 
-    @pl.when(step == 0)
-    def _():
-        for k in range(STEPS):
-            for copy in loads(k):
-                copy.start()
+    for k in range(STEPS):
+        for copy in loads(k):
+            copy.start()
+    next_load = pltpu.make_async_copy(onext_in, onext, next_sem)
+    next_load.start()
 
     spots, rights = [], []
-    for o in range(width // NB):
-        spot = [pl.ds(pl.multiple_of(place[step, 2 * o + c] * H, H), H) for c in range(2)]
+    for o in range(total // NB):
+        spot = [pl.ds(pl.multiple_of(place[2 * o + c] * H, H), H) for c in range(2)]
         spots.append(spot)
-        rights.append(jnp.concatenate([fr[:, s] * mask[0, o : o + 1, c * H : c * H + H] for c, s in enumerate(spot)], axis=1))
-
+        rights.append(jnp.concatenate([fr[:, s] * mask[o : o + 1, c * H : c * H + H] for c, s in enumerate(spot)], axis=1))
+
+    writes = []
     for k in range(STEPS):
         rows = slice(k * NB, (k + 1) * NB)
-
-        @pl.when(step == 0)
-        def _():
-            for copy in loads(k):
-                copy.wait()
-
-        spread = jnp.concatenate(
-            [
-                lax.dot_general(
-                    jnp.concatenate([fl[rows, s] for s in spot], axis=1),
-                    right,
-                    (((1,), (1,)), ((), ())),
-                    preferred_element_type=F32,
-                )
-                for spot, right in zip(spots, rights)
-            ],
-            axis=1,
-        )
-        acc = jnp.where(step == 0, op[rows, :], panel[rows, :]).astype(F32) + spread
-        if k > 0:
-            done = slice(0, k * NB)
-            acc = acc - (dot(lh[rows, done], rh[done, :]) + dot(ll[rows, done], rh[done, :]))
-        bh, bl = split(acc)
-        u = dot3(xh[rows, :], xl[rows, :], bh, bl)
-        rh[rows, :] = u.astype(BF16)
-        upper[rows, :] = u
-
-        @pl.when(step == 0)
-        def _():
-            wt[:, rows] = u.T.astype(BF16)
-
-    @pl.when(step > 0)
-    def _():
-        below[...] = onext[...].astype(F32) - dot(wt[...], rh[...])
+        for copy in loads(k):
+            copy.wait()
+        for t in range(total // tile):
+            right = slice(t * tile, (t + 1) * tile)
+            spread = jnp.concatenate(
+                [
+                    lax.dot_general(
+                        jnp.concatenate([fl[rows, s] for s in spots[o]], axis=1),
+                        rights[o],
+                        (((1,), (1,)), ((), ())),
+                        preferred_element_type=F32,
+                    )
+                    for o in range(t * tile // NB, (t + 1) * tile // NB)
+                ],
+                axis=1,
+            )
+            mine = slice(right.start - lead, right.stop - lead)
+            acc = (op[rows, right] if t == 0 else panel[rows, mine]).astype(F32) + spread
+            if k > 0:
+                done = slice(0, k * NB)
+                acc = acc - (dot(lh[rows, done], rh[done, right]) + dot(ll[rows, done], rh[done, right]))
+            bh, bl = split(acc)
+            u = dot3(xh[rows, :], xl[rows, :], bh, bl)
+            rh[rows, right] = u.astype(BF16)
+            if t == 0:
+                wt[:, rows] = u.T.astype(BF16)
+            else:
+                upper[rows, mine] = u
+        copy = pltpu.make_async_copy(upper.at[pl.ds(k * NB, NB), :], upper_out.at[pl.ds(k * NB, NB), :], out_sem.at[len(writes)])
+        copy.start()
+        writes.append(copy)
+
+    next_load.wait()
+    for t in range(width // NB):
+        right = slice(t * NB, (t + 1) * NB)
+        below[:, right] = onext[:, right].astype(F32) - dot(wt[...], rh[:, lead + t * NB : lead + (t + 1) * NB])
+        copy = pltpu.make_async_copy(below.at[:, pl.ds(t * NB, NB)], below_out.at[:, pl.ds(t * NB, NB)], out_sem.at[len(writes)])
+        copy.start()
+        writes.append(copy)
+    for copy in writes:
+        copy.wait()
 
 
 def solve_call(place, lh, ll, xh, xl, fl, fr, op, panel, mask, onext):
-    width = 512
-    count = panel.shape[1] // width
     any_spec = pl.BlockSpec(memory_space=pl.ANY)
-
-    def whole(x):
-        return pl.BlockSpec(x.shape, lambda t, p: (0, 0), pipeline_mode=pl.Buffered(1))
-
-    def tile(x):
-        return pl.BlockSpec((x.shape[0], width), lambda t, p: (0, jnp.maximum(t - 1, 0)))
-
+    vmem = pl.BlockSpec(memory_space=pltpu.VMEM)
+    dma = pltpu.SemaphoreType.DMA
+    width = panel.shape[1]
     return pl.pallas_call(
         solve_kernel,
         out_shape=(
             jax.ShapeDtypeStruct(panel.shape, F32),
             jax.ShapeDtypeStruct(onext.shape, F32),
         ),
-        grid_spec=pltpu.PrefetchScalarGridSpec(
-            num_scalar_prefetch=1,
-            grid=(count + 1,),
-            in_specs=[any_spec] * 4
-            + [whole(x) for x in (xh, xl, fr)]
-            + [tile(panel), pl.BlockSpec((1, 2, 2 * H), lambda t, p: (t, 0, 0)), tile(onext)],
-            out_specs=(tile(panel), tile(onext)),
-            scratch_shapes=[
-                pltpu.VMEM((N, N), BF16),
-                pltpu.VMEM((N, N), BF16),
-                pltpu.VMEM((N, 1024), BF16),
-                pltpu.VMEM((N, 512), BF16),
-                pltpu.VMEM((N, width), BF16),
-                pltpu.VMEM((512, N), BF16),
-                pltpu.SemaphoreType.DMA((STEPS, 4)),
-            ],
-        ),
+        in_specs=[pl.BlockSpec(memory_space=pltpu.SMEM)] + [any_spec] * 6 + [vmem] * 4,
+        out_specs=(any_spec, any_spec),
+        scratch_shapes=[
+            pltpu.VMEM((N, N), BF16),
+            pltpu.VMEM((N, N), BF16),
+            pltpu.VMEM(fl.shape, BF16),
+            pltpu.VMEM(op.shape, BF16),
+            pltpu.VMEM(panel.shape, BF16),
+            pltpu.VMEM(onext.shape, BF16),
+            pltpu.VMEM((N, op.shape[1] + width), BF16),
+            pltpu.VMEM((op.shape[1], N), BF16),
+            pltpu.VMEM(panel.shape, F32),
+            pltpu.VMEM(onext.shape, F32),
+            dma((STEPS, 5)),
+            dma(()),
+            dma((STEPS + width // NB,)),
+        ],
         compiler_params=pltpu.CompilerParams(vmem_limit_bytes=56 << 20),
         name="solve",
-    )(place, lh, ll, fl, op, xh, xl, fr, panel, mask, onext)
+    )(place, lh, ll, fl, op, panel, onext, xh, xl, fr, mask)
 
 
 def shards(fac_left, fac_right, block_rank, col_map, child_lead, orig_lead, orig_panel, orig_next):
@@ -494,10 +522,10 @@
     ranks = lax.dynamic_slice_in_dim(block_rank, leaf - par, 2, 0).reshape(16)
     hit = (targets[:, None] == maps[None, :]).reshape(6, 2, 8)
     pair = jnp.sum(jnp.where(hit, jnp.arange(8, dtype=jnp.int32) // 2, 0), axis=2)
-    place = (pair + jnp.array([[0, 4]], jnp.int32)).reshape(3, 4)
+    place = (pair + jnp.array([[0, 4]], jnp.int32)).reshape(12)
     live = (jnp.arange(RMAX)[None, :] < ranks[:, None]).reshape(1, 2, 8, RMAX)
     used = (hit[..., None] & live).reshape(6, 2, 4, 2 * RMAX)
-    mask = jnp.any(used, axis=2).astype(BF16).reshape(3, 2, 4 * RMAX)
+    mask = jnp.any(used, axis=2).astype(BF16).reshape(6, 4 * RMAX)
     upper, below = solve_call(place, lh, ll, xh, xl, flg, frg, opg, orig_panel[0], mask, orig_next[0])
     return (out_lead[None], upper[None], below[None])
 

time: 120 us -> 113 us (0.942)
  Pallas kernels: 114 us -> 108 us
    pallas_call x1, Pallas kernels: 26.9 us -> 21 us  [solve_call(): pl.pallas_call(solve_kernel, out_shape=(jax.ShapeDtypeStruct(panel.shape,...]
where the time goes in v5:
time: 113 us
  Pallas kernels  108 us (96%)
  local copies, waits for them, and re-layouts  4.02 us (4%)
    pallas_call x1, Pallas kernels, factor_call(): pl.pallas_call(factor_kernel, out_shape=(jax.ShapeDtypeStruct((QUARTER, N...  86.5 us
    pallas_call x1, Pallas kernels, solve_call(): pl.pallas_call(solve_kernel, out_shape=(jax.ShapeDtypeStruct(panel.shape,...  21 us

profile of v5, /device:TPU:0, one launch (start us, length us, event | category | flops | bytes accessed | tf_op | source)
XLA Modules:
  0.0 112.8 jit_solution(17809012106615561024)
XLA Ops:
  0.7 0.1 pad_add_fusion
  0.8 0.1 lt.36
  0.8 0.8 constant_dynamic-slice_fusion
  1.6 0.1 copy.18
  1.7 0.1 copy.17
  1.8 0.1 broadcast_compare_fusion
  1.9 0.2 select_reduce_fusion
  2.1 0.7 add.40.place
  2.8 0.1 lt.38
  2.9 0.1 lt.39
  2.9 0.1 and.30
  3.0 0.1 and.31
  3.2 0.6 copy.21
  3.8 86.5 %factor.1 = (f32[384,1536]{1,0:T(8,128)}, bf16[1536,1536]{1,0:T(8,128)(2,1)}, bf16[1536,1536]{1,0:T(8,128)(2,1)}, bf16[1536,256]{1,0:T(8,128)(2,1)}, bf16[1536,2...) custom-call(bf16[768,1536]{1,0:T(8,128)(2,1)} %bitcast.19, ...), custom_call_target="tpu_custom_call" | custom-call | tf_op jit(solution)/shard_map/factor/pallas_call | solution.py:368
  90.3 0.0 copy-start
  90.3 21.0 %solve.1 = (f32[1536,1024]{1,0:T(8,128)}, f32[512,1024]{1,0:T(8,128)}) custom-call(s32[12]{0:T(128)} %add.40.place, bf16[1536,1536]{1,0:T(8,128)(2,1)} %get-tuple-element.14.lh_in, bf16[1536,1536]{1,0:T(8,128)(2,1)} %get-tuple-element.15.ll_in, bf16[1536,1024]{1,0:T(8,128)(2,1)} %get-tuple-element.16.fl_in, bf16[1536,512]{1,0:T(8,128)(2,1)} %get-tuple-element.17.op_in, ...), custom_call_target="tpu_custom_call" | custom-call | tf_op jit(solution)/shard_map/solve/pallas_call | solution.py:485
  111.4 0.0 copy-done
  111.4 1.4 %copy.23 = f32[1,384,1536]{2,1,0:T(8,128)} copy(f32[1,384,1536]{2,1,0:T(8,128)S(1)} %bitcast.18) | data formatting | bytes 4718592
  (9 shorter events, 0.1 us)
Async XLA Ops:
  90.3 21.1 %copy-start = (f32[384,1536]{1,0:T(8,128)S(1)}, f32[384,1536]{1,0:T(8,128)}, u32[]{:S(2)}) copy-start(f32[384,1536]{1,0:T(8,128)} %get-tuple-element.13) | copy-start | bytes 7077892

commit v6 on v5

--- a/solution.py
+++ b/solution.py
@@ -93,8 +93,8 @@
 
 def factor_kernel(
     child, orig, fl, fr, op,
-    out_lead, lh_out, ll_out, xh, xl, flg, frg, opg,
-    ca, cb, og, ox, acol, lf, lh, ll, uh, ul, xf, r_ref, w_ref, u_a, x_a, u_b, x_b, held,
+    out_lead, lh_out, ll_out, xh, xl, fl_out, fr_out, op_out,
+    ca, cb, og, ox, acol, lf, lh, ll, uh, ul, xf, r_ref, w_ref, u_a, x_a, u_b, x_b, held, flg, frg, opg,
     loc, sib_send, sib_recv, x_send, relay_send, x_recv, out_sem,
 ):
     leaf, core = lax.axis_index("leaf"), lax.axis_index("front")
@@ -121,11 +121,7 @@
     own_col, cross_col, cross = [], [], []
     for k in range(STEPS):
         own_col.append([len(own)])
-        high = min(NB * (k + 1), HALF)
-        own.append((0, box(child, 0, high, k * NB, NB), box(ca, 0, high, k * NB, NB)))
-        if k >= 3:
-            own_col[k].append(len(own))
-            own.append((1, box(child, 0, NB * (k - 2), k * NB, NB), box(ca, HALF, NB * (k - 2), k * NB, NB)))
+        own.append((k // 3, box(child, k % 3 * NB, NB, k * NB, N - k * NB), box(ca, k * NB, NB, k * NB, N - k * NB)))
     own_fac = tuple(range(len(own), len(own) + 5))
     for c in range(2):
         own.append((c, fl, slot(flg, 2 * par + c, 256)))
@@ -276,19 +272,24 @@
 
     AHEAD = 2
     writes = []
+
+    def hand_over(half):
+        for ref, dst, width in ((flg, fl_out, 512), (frg, fr_out, 512), (opg, op_out, NB)):
+            copy = pltpu.make_async_copy(slot(ref, half, width), slot(dst, half, width), out_sem.at[len(writes)])
+            copy.start()
+            writes.append(copy)
+
     for k in range(STEPS):
         rows = slice(k * NB, (k + 1) * NB)
         if k <= AHEAD:
             ready(k)
-        if k == 0:
-            start_cross(*cross_col[2])
-        if k == 1:
-            start_cross(*cross_col[4])
         if k == 2:
-            start_cross(*cross_fl)
             start_own(*own_fac)
         if k == 3:
             start_cross(*cross_rest)
+        if k == 4:
+            wait_own(*own_fac)
+            hand_over(par)
         if AHEAD <= k < STEPS - 1:
             pass_on(*cross_col[k + 1])
 
@@ -309,13 +310,11 @@
                 writes.append(copy)
         factor_128(r_ref, w_ref, u_a, x_a, held)
         if k == 0:
-            start_cross(*cross_col[3])
+            start_cross(*cross_col[2])
         if k == 1:
-            start_cross(*cross_col[5])
-        if k < AHEAD:
-            pass_on(*cross_col[k + 1])
-        if k == STEPS - 1:
-            pass_on(*cross_fl)
+            start_cross(*cross_col[4])
+        if k == 2:
+            start_cross(*cross_fl)
         if AHEAD <= k < STEPS - 1:
             ready(k + 1)
         mid = rows.start + H
@@ -329,8 +328,11 @@
             for i in range(k):
                 eliminate(k + 1, i)
         factor_128(r_ref, w_ref, u_b, x_b, held)
+        if k < AHEAD:
+            pass_on(*cross_col[k + 1])
+            start_cross(*cross_col[3 + 2 * k])
         if k == STEPS - 1:
-            pass_on(*cross_rest)
+            pass_on(*cross_fl, *cross_rest)
         xf[0:H, 0:H] = xa
         xf[0:H, H:NB] = jnp.zeros((H, H), F32)
         xf[H:NB, 0:H] = -dot_split(x_b[...], below_a)
@@ -346,8 +348,8 @@
     write = pltpu.make_async_copy(lf.at[mine, :], out_lead, out_sem.at[len(writes)])
     write.start()
     writes.append(write)
-    wait_own(*own_fac)
     take(*cross_fl, *cross_rest)
+    hand_over(1 - par)
     for n in range(len(own)):
         @pl.when(core == own[n][0])
         def _():
@@ -394,7 +396,8 @@
         ]
         + [pltpu.VMEM((H, H), F32)] * 6
         + [pltpu.VMEM((W * W, H), F32)]
-        + [dma((18,)), dma((18,)), dma((18,)), dma((19,)), dma((19,)), dma((19,)), dma((11,))],
+        + [pltpu.VMEM((N, 1024), BF16), pltpu.VMEM((NB, 1024), BF16), pltpu.VMEM((N, 512), BF16)]
+        + [dma((15,)), dma((15,)), dma((15,)), dma((19,)), dma((19,)), dma((19,)), dma((17,))],
         compiler_params=pltpu.CompilerParams(
             collective_id=0, has_side_effects=True, vmem_limit_bytes=56 << 20
         ),

time: 113 us -> 110 us (0.973)
  the two profiles are of different devices: /device:TPU:0 before, /device:TPU:1 now
where the time goes in v6:
time: 110 us
  Pallas kernels  105 us (95%)
  local copies, waits for them, and re-layouts  4.02 us (4%)
    pallas_call x1, Pallas kernels, factor_call(): pl.pallas_call(factor_kernel, out_shape=(jax.ShapeDtypeStruct((QUARTER, N...  83.9 us
    pallas_call x1, Pallas kernels, solve_call(): pl.pallas_call(solve_kernel, out_shape=(jax.ShapeDtypeStruct(panel.shape,...  21 us

profile of v6, /device:TPU:1, one launch (start us, length us, event | category | flops | bytes accessed | tf_op | source)
XLA Modules:
  0.0 110.1 jit_solution(10095297391231506140)
XLA Ops:
  0.7 0.1 pad_add_fusion
  0.8 0.1 lt.36
  0.8 0.8 constant_dynamic-slice_fusion
  1.6 0.1 copy.18
  1.7 0.1 copy.17
  1.8 0.1 broadcast_compare_fusion
  1.9 0.2 select_reduce_fusion
  2.1 0.7 add.40.place
  2.8 0.1 lt.38
  2.9 0.1 lt.39
  2.9 0.1 and.30
  3.0 0.1 and.31
  3.2 0.6 copy.21
  3.8 83.9 %factor.1 = (f32[384,1536]{1,0:T(8,128)}, bf16[1536,1536]{1,0:T(8,128)(2,1)}, bf16[1536,1536]{1,0:T(8,128)(2,1)}, bf16[1536,256]{1,0:T(8,128)(2,1)}, bf16[1536,2...) custom-call(bf16[768,1536]{1,0:T(8,128)(2,1)} %bitcast.19, ...), custom_call_target="tpu_custom_call" | custom-call | tf_op jit(solution)/shard_map/factor/pallas_call | solution.py:370
  87.7 0.0 copy-start
  87.7 21.0 %solve.1 = (f32[1536,1024]{1,0:T(8,128)}, f32[512,1024]{1,0:T(8,128)}) custom-call(s32[12]{0:T(128)} %add.40.place, bf16[1536,1536]{1,0:T(8,128)(2,1)} %get-tuple-element.14.lh_in, bf16[1536,1536]{1,0:T(8,128)(2,1)} %get-tuple-element.15.ll_in, bf16[1536,1024]{1,0:T(8,128)(2,1)} %get-tuple-element.16.fl_in, bf16[1536,512]{1,0:T(8,128)(2,1)} %get-tuple-element.17.op_in, ...), custom_call_target="tpu_custom_call" | custom-call | tf_op jit(solution)/shard_map/solve/pallas_call | solution.py:488
  108.7 0.0 copy-done
  108.7 1.4 %copy.23 = f32[1,384,1536]{2,1,0:T(8,128)} copy(f32[1,384,1536]{2,1,0:T(8,128)S(1)} %bitcast.18) | data formatting | bytes 4718592
  (9 shorter events, 0.1 us)
Async XLA Ops:
  87.7 21.1 %copy-start = (f32[384,1536]{1,0:T(8,128)S(1)}, f32[384,1536]{1,0:T(8,128)}, u32[]{:S(2)}) copy-start(f32[384,1536]{1,0:T(8,128)} %get-tuple-element.13) | copy-start | bytes 7077892

commit v7 on v6

--- a/solution.py
+++ b/solution.py
@@ -406,7 +406,7 @@
 
 
 def solve_kernel(
-    place, lh_in, ll_in, fl_in, op_in, panel_in, onext_in, xh, xl, fr, mask, upper_out, below_out,
+    maps, ranks, lh_in, ll_in, fl_in, op_in, panel_in, onext_in, xh, xl, fr, upper_out, below_out,
     lh, ll, fl, op, panel, onext, rh, wt, upper, below, sems, next_sem, out_sem,
 ):
     lead, width = op.shape[1], panel.shape[1]
@@ -428,11 +428,25 @@
     next_load = pltpu.make_async_copy(onext_in, onext, next_sem)
     next_load.start()
 
+    leaf, core = lax.axis_index("leaf"), lax.axis_index("front")
+    par = lax.rem(leaf, 2)
+    lane = lax.broadcasted_iota(jnp.int32, (1, H), 1)
     spots, rights = [], []
     for o in range(total // NB):
-        spot = [pl.ds(pl.multiple_of(place[2 * o + c] * H, H), H) for c in range(2)]
+        target = 8 * o if o < 2 else par * 8 + core * 4 + (o - 2)
+        spot, pieces = [], []
+        for c in range(2):
+            block, rank = jnp.int32(0), jnp.int32(0)
+            for n in range(8):
+                hit = maps[leaf - par + c, n] == target
+                block = jnp.where(hit, n, block)
+                rank = jnp.where(hit, ranks[leaf - par + c, n], rank)
+            low = lax.rem(block, 2) * RMAX
+            used = jnp.where((lane >= low) & (lane < low + rank), 1.0, 0.0).astype(BF16)
+            spot.append(pl.ds(pl.multiple_of((4 * c + lax.div(block, 2)) * H, H), H))
+            pieces.append(fr[:, spot[c]] * used)
         spots.append(spot)
-        rights.append(jnp.concatenate([fr[:, s] * mask[o : o + 1, c * H : c * H + H] for c, s in enumerate(spot)], axis=1))
+        rights.append(jnp.concatenate(pieces, axis=1))
 
     writes = []
     for k in range(STEPS):
@@ -480,7 +494,7 @@
         copy.wait()
 
 
-def solve_call(place, lh, ll, xh, xl, fl, fr, op, panel, mask, onext):
+def solve_call(maps, ranks, lh, ll, xh, xl, fl, fr, op, panel, onext):
     any_spec = pl.BlockSpec(memory_space=pl.ANY)
     vmem = pl.BlockSpec(memory_space=pltpu.VMEM)
     dma = pltpu.SemaphoreType.DMA
@@ -491,7 +505,7 @@
             jax.ShapeDtypeStruct(panel.shape, F32),
             jax.ShapeDtypeStruct(onext.shape, F32),
         ),
-        in_specs=[pl.BlockSpec(memory_space=pltpu.SMEM)] + [any_spec] * 6 + [vmem] * 4,
+        in_specs=[pl.BlockSpec(memory_space=pltpu.SMEM)] * 2 + [any_spec] * 6 + [vmem] * 3,
         out_specs=(any_spec, any_spec),
         scratch_shapes=[
             pltpu.VMEM((N, N), BF16),
@@ -510,26 +524,14 @@
         ],
         compiler_params=pltpu.CompilerParams(vmem_limit_bytes=56 << 20),
         name="solve",
-    )(place, lh, ll, fl, op, panel, onext, xh, xl, fr, mask)
+    )(maps, ranks, lh, ll, fl, op, panel, onext, xh, xl, fr)
 
 
 def shards(fac_left, fac_right, block_rank, col_map, child_lead, orig_lead, orig_panel, orig_next):
-    leaf, core = lax.axis_index("leaf"), lax.axis_index("front")
-    par = leaf % 2
     out_lead, lh, ll, xh, xl, flg, frg, opg = factor_call(
         child_lead[0], orig_lead[0], fac_left[0], fac_right[0], orig_panel[0]
     )
-    own = par * 8 + core * 4 + jnp.arange(4, dtype=jnp.int32)
-    targets = jnp.concatenate([jnp.array([0, 8], jnp.int32), own])
-    maps = lax.dynamic_slice_in_dim(col_map, leaf - par, 2, 0).reshape(16)
-    ranks = lax.dynamic_slice_in_dim(block_rank, leaf - par, 2, 0).reshape(16)
-    hit = (targets[:, None] == maps[None, :]).reshape(6, 2, 8)
-    pair = jnp.sum(jnp.where(hit, jnp.arange(8, dtype=jnp.int32) // 2, 0), axis=2)
-    place = (pair + jnp.array([[0, 4]], jnp.int32)).reshape(12)
-    live = (jnp.arange(RMAX)[None, :] < ranks[:, None]).reshape(1, 2, 8, RMAX)
-    used = (hit[..., None] & live).reshape(6, 2, 4, 2 * RMAX)
-    mask = jnp.any(used, axis=2).astype(BF16).reshape(6, 4 * RMAX)
-    upper, below = solve_call(place, lh, ll, xh, xl, flg, frg, opg, orig_panel[0], mask, orig_next[0])
+    upper, below = solve_call(col_map, block_rank, lh, ll, xh, xl, flg, frg, opg, orig_panel[0], orig_next[0])
     return (out_lead[None], upper[None], below[None])
 
 

time: 110 us -> 110 us (level)
    unnamed x4 -> x5, local copies, waits for them, and re-layouts: 2.01 us -> 4.17 us
where the time goes in v7:
time: 110 us
  Pallas kernels  105 us (95%)
  local copies, waits for them, and re-layouts  4.17 us (4%)
    pallas_call x1, Pallas kernels, factor_call(): pl.pallas_call(factor_kernel, out_shape=(jax.ShapeDtypeStruct((QUARTER, N...  83.8 us
    pallas_call x1, Pallas kernels, solve_call(): pl.pallas_call(solve_kernel, out_shape=(jax.ShapeDtypeStruct(panel.shape,...  21.2 us
    unnamed x5, local copies, waits for them, and re-layouts  4.17 us

profile of v7, /device:TPU:1, one launch (start us, length us, event | category | flops | bytes accessed | tf_op | source)
XLA Modules:
  0.0 109.8 jit_solution(18244248098586686447)
XLA Ops:
  0.6 1.4 %copy.12.ranks = s32[64,8]{1,0:T(8,128)} copy(s32[64,8]{0,1:T(8,128)} %param.10) | data formatting | bytes 4096 | tf_op args[2]
  2.0 1.4 %copy.11.maps = s32[64,8]{1,0:T(8,128)} copy(s32[64,8]{0,1:T(8,128)} %param.11) | data formatting | bytes 4096 | tf_op args[3]
  3.4 83.8 %factor.1 = (f32[384,1536]{1,0:T(8,128)}, bf16[1536,1536]{1,0:T(8,128)(2,1)}, bf16[1536,1536]{1,0:T(8,128)(2,1)}, bf16[1536,256]{1,0:T(8,128)(2,1)}, bf16[1536,2...) custom-call(bf16[768,1536]{1,0:T(8,128)(2,1)} %bitcast.12, ...), custom_call_target="tpu_custom_call" | custom-call | tf_op jit(solution)/shard_map/factor/pallas_call | solution.py:370
  87.2 0.0 copy-start
  87.2 21.2 %solve.1 = (f32[1536,1024]{1,0:T(8,128)}, f32[512,1024]{1,0:T(8,128)}) custom-call(s32[64,8]{1,0:T(8,128)} %copy.11.maps, s32[64,8]{1,0:T(8,128)} %copy.12.ranks, bf16[1536,1536]{1,0:T(8,128)(2,1)} %get-tuple-element.14.lh_in, bf16[1536,1536]{1,0:T(8,128)(2,1)} %get-tuple-element.15.ll_in, bf16[1536,1024]{1,0:T(8,128)(2,1)} %get-tuple-element.16.fl_in, ...), custom_call_target="tpu_custom_call" | custom-call | tf_op jit(solution)/shard_map/solve/pallas_call | solution.py:502
  108.4 0.0 copy-done
  108.4 1.4 %copy.14 = f32[1,384,1536]{2,1,0:T(8,128)} copy(f32[1,384,1536]{2,1,0:T(8,128)S(1)} %bitcast.11) | data formatting | bytes 4718592
Async XLA Ops:
  87.2 21.2 %copy-start = (f32[384,1536]{1,0:T(8,128)S(1)}, f32[384,1536]{1,0:T(8,128)}, u32[]{:S(2)}) copy-start(f32[384,1536]{1,0:T(8,128)} %get-tuple-element.13) | copy-start | bytes 7077892
